TPU v7x, 32 devices: a whole 2x2x4 slice. The times are simulated.
32 devices in a mesh: region: 8 (over z, y), lev: 4 (over x, core).
Axes of the slice: x: 2, y: 2, z: 4, core: 2. Of those that a mesh axis runs over, the one named last changes fastest.
Arguments:
- background_members: bfloat16 [80, 16, 1024, 8], P(None, 'lev', 'region'), may hold values from -6 to 6
- channel_height_kernel: float32 [8, 16], P(None, 'lev'), may hold values from -1.5 to 1.5
- sensor_spread_down: float32 [4], replicated, may hold values from 0.2 to 0.6
- sensor_spread_across: float32 [4], replicated, may hold values from 0.2 to 0.6
- measurement_placement: int32 [4, 64], replicated, may hold values from 0 to 511
- measurement_ordering: int32 [4, 64], replicated, may hold values from 0 to 63, each once within a row
- group_area_number: int32 [4], replicated, may hold values from 0 to 7
- taper_radius_limit: int32 [8], replicated, may hold values from 8 to 16
- measured_amounts: float32 [4, 64], replicated, may hold values from -8 to 8
- measurement_noise_spread: float32 [4, 64], replicated, may hold values from 0.05 to 0.5
Outputs:
- analysis: bfloat16 [80, 16, 8, 1024], P(None, 'lev', 'region')
All inputs are finite; a program needn't handle non-finite values.
Results may differ from a plain program's by a relative error of at most 0.001.
Values may be sent and summed in bfloat16 or wider, within the bound.
No kernel may reach another device: no remote copies, remote signals or barrier semaphores. Data moves between devices by JAX's collectives and lax.ppermute only.
A program may use at most 128 MiB of HBM per device.

v0:
```python
import jax
import jax.numpy as jnp
from jax import lax
from jax.sharding import PartitionSpec as P

TILE = 32
STRIDE = 4


highest = lax.Precision.HIGHEST
group_width = 32


def footprint(present_state_grid, sensor_spread_down, sensor_spread_across, channel_height_kernel):
    members, levels, pixels = present_state_grid.shape
    foot_cells = TILE // STRIDE
    tiles_view = present_state_grid.reshape(members, levels, foot_cells, STRIDE, foot_cells, STRIDE)
    blocks = jnp.einsum(
        "klaicj,i,j->klac", tiles_view, sensor_spread_down, sensor_spread_across, precision=highest
    )
    blocks = blocks.reshape(members, levels, foot_cells * foot_cells)
    weighted = jnp.einsum("klq,hl->khq", blocks, channel_height_kernel, precision=highest)
    return weighted.reshape(members, -1)


def taper_weight(distance, cut_radius):
    return jnp.maximum(0.0, 1.0 - distance / (cut_radius + 1.0))


def serial_block(current, values, errors):
    denominator = current.shape[0] - 1.0
    recorded = []
    for column_id in range(current.shape[1]):
        column = current[:, column_id]
        center_col = jnp.mean(column)
        anomaly_col = column - center_col
        variance = jnp.sum(anomaly_col * anomaly_col) / denominator + errors[column_id]
        alpha_gain = 1.0 / (1.0 + jnp.sqrt(errors[column_id] / variance))
        innovation = values[column_id] - center_col
        recorded.append(column)
        anomaly_all = current - jnp.mean(current, axis=0, keepdims=True)
        covariance = jnp.dot(anomaly_col, anomaly_all, precision=highest) / denominator
        current = current + jnp.outer(innovation - alpha_gain * anomaly_col, covariance / variance)
    return jnp.stack(recorded, axis=1)


def block_terms(recorded, values, errors):
    denominator = recorded.shape[0] - 1.0
    center_blk = jnp.mean(recorded, axis=0)
    anomaly_rec = recorded - center_blk[None]
    variance = jnp.sum(anomaly_rec * anomaly_rec, axis=0) / denominator + errors
    alpha_gain = 1.0 / (1.0 + jnp.sqrt(errors / variance))
    scale_pert = alpha_gain / (denominator * variance)
    scale_mean = (values - center_blk) / (denominator * variance)
    return (anomaly_rec, scale_pert, scale_mean)


def advance(transforms, offsets, anomaly_rec, scale_pert, scale_mean, tapers):
    block_size = anomaly_rec.shape[1]
    gram_matrix = jnp.dot(anomaly_rec.T, anomaly_rec, precision=highest)
    upper_part = jnp.triu(gram_matrix, 1)
    coef_pert = tapers * scale_pert[None]
    coef_mean = tapers * scale_mean[None]
    identity_blk = jnp.eye(block_size, dtype=jnp.float32)[None]
    nilpotent = coef_pert[:, :, None] * upper_part[None]
    inverse = identity_blk - nilpotent
    power = nilpotent
    for level_id in range((block_size - 1).bit_length() - 1):
        power = jnp.einsum("tij,tjk->tik", power, power, precision=highest)
        inverse = inverse + jnp.einsum("tij,tjk->tik", inverse, power, precision=highest)
    factor = inverse * coef_pert[:, None, :]
    carried = jnp.einsum("ij,tj->ti", upper_part, coef_mean, precision=highest)
    weights_mean = coef_mean - jnp.einsum("tij,tj->ti", factor, carried, precision=highest)
    mapped = jnp.einsum("tkm,mj->tkj", transforms, anomaly_rec, precision=highest)
    offsets = offsets + jnp.einsum("tkj,tj->tk", mapped, weights_mean, precision=highest)
    folded = jnp.einsum("tkj,tjl->tkl", mapped, factor, precision=highest)
    transforms = transforms - jnp.einsum("tkl,ml->tkm", folded, anomaly_rec, precision=highest)
    return (transforms, offsets)


def run_batch(base_priors, values, errors, transforms, offsets, tapers, target):
    center = jnp.mean(base_priors, axis=0)
    anomaly = base_priors - center[None]
    count_blocks = base_priors.shape[1] // group_width

    def one_block(block_id, state_carry):
        transforms, offsets, recorded_all = state_carry
        start = block_id * group_width
        anomaly_blk = lax.dynamic_slice_in_dim(anomaly, start, group_width, 1)
        center_blk = lax.dynamic_slice_in_dim(center, start, group_width, 0)
        values_blk = lax.dynamic_slice_in_dim(values, start, group_width, 0)
        errors_blk = lax.dynamic_slice_in_dim(errors, start, group_width, 0)
        tapers_blk = lax.dynamic_slice_in_dim(tapers, start, group_width, 1)
        current = (
            jnp.dot(transforms[target].T, anomaly_blk, precision=highest)
            + (center_blk + jnp.dot(offsets[target], anomaly_blk, precision=highest))[None]
        )
        recorded = serial_block(current, values_blk, errors_blk)
        anomaly_rec, scale_pert, scale_mean = block_terms(recorded, values_blk, errors_blk)
        transforms, offsets = advance(
            transforms, offsets, anomaly_rec, scale_pert, scale_mean, tapers_blk
        )
        recorded_all = lax.dynamic_update_slice_in_dim(recorded_all, recorded, start, 1)
        return (transforms, offsets, recorded_all)

    return lax.fori_loop(
        0, count_blocks, one_block, (transforms, offsets, jnp.zeros_like(base_priors))
    )


def body(
    background_members,
    channel_height_kernel,
    sensor_spread_down,
    sensor_spread_across,
    measurement_placement,
    measurement_ordering,
    group_area_number,
    taper_radius_limit,
    measured_amounts,
    measurement_noise_spread,
):
    own_region = lax.axis_index("region")
    present_state_grid = lax.all_to_all(
        background_members, "region", split_axis=3, concat_axis=2, tiled=True
    )[:, :, :, 0].astype(jnp.float32)
    present_state_grid, partial_priors = (
        present_state_grid,
        footprint(
            present_state_grid, sensor_spread_down, sensor_spread_across, channel_height_kernel
        ),
    )
    priors = lax.psum(partial_priors, "lev")
    members, levels, pixels = present_state_grid.shape
    flat_field = present_state_grid.reshape(members, levels * pixels)
    center = jnp.mean(flat_field, axis=0)
    anomaly = flat_field - center[None]
    picked = jnp.take_along_axis(measurement_placement, measurement_ordering, axis=1)
    values_all = jnp.take_along_axis(measured_amounts, measurement_ordering, axis=1)
    errors_all = jnp.take_along_axis(measurement_noise_spread, measurement_ordering, axis=1)
    foot_cells = TILE // STRIDE * (TILE // STRIDE)
    channels = picked // foot_cells
    channel_ids = jnp.arange(taper_radius_limit.shape[0], dtype=jnp.int32)
    cut_radius = jnp.sum(
        jnp.where(channels[:, :, None] == channel_ids, taper_radius_limit, 0), axis=2
    ).astype(jnp.float32)
    batches = measurement_placement.shape[0]
    eye_members = jnp.eye(members, dtype=jnp.float32)
    hosting = own_region == group_area_number
    chosen = jnp.take(priors, picked.reshape(-1), axis=1).reshape(members, batches, -1)
    chosen = jnp.where(hosting[None, :, None], chosen, 0.0)
    bases = lax.psum(chosen, "region")
    targets = jnp.concatenate([own_region[None], group_area_number])
    count_targets = batches + 1
    transforms = jnp.tile(eye_members[None], (count_targets, 1, 1))
    offsets = jnp.zeros((count_targets, members), jnp.float32)
    for batch_id in range(batches):
        distance = jnp.abs(targets - group_area_number[batch_id]).astype(jnp.float32)
        tapers = taper_weight(distance[:, None], cut_radius[batch_id][None])
        outcome = run_batch(
            bases[:, batch_id],
            values_all[batch_id],
            errors_all[batch_id],
            transforms,
            offsets,
            tapers,
            1 + batch_id,
        )
        transforms, offsets = (outcome[0], outcome[1])
    mixing = transforms[0] + offsets[0][:, None]
    result = jnp.dot(mixing.T, anomaly, precision=highest) + center[None]
    return result.reshape(members, levels, 1, pixels).astype(jnp.bfloat16)


def solution(mesh):
    return jax.shard_map(
        body,
        mesh=mesh,
        in_specs=(
            P(None, "lev", "region", None),
            P(None, "lev"),
            P(),
            P(),
            P(),
            P(),
            P(),
            P(),
            P(),
            P(),
        ),
        out_specs=P(None, "lev", "region", None),
        check_vma=False,
    )
```

profile of v0, /device:TPU:0, one launch (start us, length us, event | category | flops | bytes accessed | tf_op | source)
XLA Modules:
  0.0 1444.8 jit_solution(3757707560450293175)
XLA Ops:
  6.5 2.2 copy.48
  8.8 7.5 all-to-all-start
  16.4 2.4 gather_fusion.1
  19.8 0.7 abs_convert_fusion
  20.6 1.8 abs_convert_fusion.1
  22.5 2.4 gather_fusion.3
  25.1 2.4 gather_fusion.2
  27.8 5.8 all-to-all-done
  33.5 0.7 copy.49
  34.9 0.9 multiply_reduce_fusion.4
  36.2 0.8 copy.84
  37.4 31.1 %all-reduce.3.cloned.1.call-done = f32[80,512]{0,1:T(8,128)} async-done(((f32[80,512]{0,1:T(8,128)}), f32[80,512]{0,1:T(8,128)}) %all-reduce.3.cloned.1.call-update) | async-done | bytes 163856 | tf_op jit(solution)/shard_map/psum | solution.py:133
  68.5 1.7 gather_fusion
  70.2 0.7 select_select_fusion
  71.8 1.8 copy.54
  73.6 1.5 sub.8074
  75.1 66.7 %all-reduce.5.cloned.1.call-done = f32[80,4,64]{2,0,1:T(8,128)} async-done(((f32[80,4,64]{2,0,1:T(8,128)}), f32[80,4,64]{2,0,1:T(8,128)}) %all-reduce.5.cloned.1.call-update) | async-done | bytes 81936 | tf_op jit(solution)/shard_map/psum | solution.py:152
  141.8 0.9 slice_reduce_fusion.124
  142.7 0.9 bitcast_subtract_fusion.4
  143.6 322.7 %while.64 = (s32[]{:T(128)}, f32[5,80,80]{2,1,0:T(8,128)S(1)}, f32[5,80]{1,0:T(8,128)S(1)}, f32[80,64]{1,0:T(8,128)S(1)}, f32[64]{0:T(128)S(1)}, /*index=5*/f32[...) while((s32[]{:T(128)}, f32[5,80,80]{2,1,0:T(8,128)S(1)}, ...), condition=%wide.region_100.102_spmd.clone, body=%wide.region_4.101_spmd.clone.sunk | while | flops 50354160 | bytes 2541750 | solution.py:106
  144.0 0.7 fusion.2380
  144.7 0.7 fusion.2376
  145.4 0.7 fusion.2414
  146.1 0.7 fusion.2418
  191.3 0.7 slice_reduce_fusion.354
  305.3 0.7 fusion.2380
  306.0 0.7 fusion.2376
  306.7 0.7 fusion.2414
  307.5 0.7 fusion.2418
  352.6 0.7 slice_reduce_fusion.354
  466.3 323.2 %while.61 = (s32[]{:T(128)}, f32[5,80,80]{2,1,0:T(8,128)S(1)}, f32[5,80]{1,0:T(8,128)S(1)}, f32[80,64]{1,0:T(8,128)S(1)}, f32[64]{0:T(128)S(1)}, /*index=5*/f32[...) while((s32[]{:T(128)}, f32[5,80,80]{2,1,0:T(8,128)S(1)}, ...), condition=%wide.region_198.200_spmd, body=%wide.region_102.199_spmd.sunk | while | flops 50353360 | bytes 2538531 | solution.py:106
  467.2 0.7 fusion.1876
  467.9 0.7 fusion.1872
  468.6 0.7 fusion.1910
  469.3 0.7 fusion.1914
  514.5 0.7 slice_reduce_fusion.261
  628.5 0.7 fusion.1876
  629.2 0.7 fusion.1872
  629.9 0.7 fusion.1910
  630.6 0.7 fusion.1914
  675.8 0.7 slice_reduce_fusion.261
  789.5 322.8 %while.62 = (s32[]{:T(128)}, f32[5,80,80]{2,1,0:T(8,128)S(1)}, f32[5,80]{1,0:T(8,128)S(1)}, f32[80,64]{1,0:T(8,128)S(1)}, f32[64]{0:T(128)S(1)}, /*index=5*/f32[...) while((s32[]{:T(128)}, f32[5,80,80]{2,1,0:T(8,128)S(1)}, ...), condition=%wide.region_296.298_spmd, body=%wide.region_200.297_spmd.sunk | while | flops 50353360 | bytes 2538531 | solution.py:106
  790.0 0.7 fusion.2044
  790.7 0.7 fusion.2040
  791.4 0.7 fusion.2078
  792.1 0.7 fusion.2082
  837.3 0.7 slice_reduce_fusion.292
  951.3 0.7 fusion.2044
  952.0 0.7 fusion.2040
  952.7 0.7 fusion.2078
  953.4 0.7 fusion.2082
  998.6 0.7 slice_reduce_fusion.292
  1112.3 322.9 %while.63 = (s32[]{:T(128)}, f32[5,80,80]{2,1,0:T(8,128)S(1)}, f32[5,80]{1,0:T(8,128)S(1)}, f32[80,64]{1,0:T(8,128)S(1)}, f32[64]{0:T(128)S(1)}, /*index=5*/f32[...) while((s32[]{:T(128)}, f32[5,80,80]{2,1,0:T(8,128)S(1)}, ...), condition=%wide.region_394.396_spmd, body=%wide.region_298.395_spmd.sunk | while | flops 50353360 | bytes 2538531 | solution.py:106
  1112.9 0.7 fusion.2212
  1113.6 0.7 fusion.2208
  1114.3 0.7 fusion.2246
  1115.0 0.7 fusion.2250
  1160.1 0.7 slice_reduce_fusion.323
  1274.2 0.7 fusion.2212
  1274.9 0.7 fusion.2208
  1275.6 0.7 fusion.2246
  1276.3 0.7 fusion.2250
  1435.1 1.3 fusion.888
  1436.5 1.3 convert_element_type.110
  (1770 shorter events, 457.7 us)
Async XLA Ops:
  6.5 29.2 %copy-start = (f32[8,4]{0,1:T(4,128)S(1)}, f32[8,4]{0,1:T(4,128)}, u32[]{:S(2)}) copy-start(f32[8,4]{0,1:T(4,128)} %param.21) | copy-start | bytes 388
  6.5 9.8 copy-start.5
  6.5 9.9 copy-start.1
  8.8 10.3 copy-start.4
  8.8 11.0 copy-start.7
  8.8 11.0 copy-start.8
  8.8 11.7 copy-start.6
  8.8 13.8 copy-start.2
  8.8 24.7 %all-to-all-start = ((bf16[80,4,128,8]{2,0,1,3:T(8,128)(2,1)}), bf16[80,4,128,8]{2,0,1,3:T(8,128)(2,1)S(1)}, u32[]{:S(2)}, u32[]{:S(2)}) async-start(bf16[80,4,128,8]{2,0,1,3:T(8,128)(2,1)} %copy.48), calls=%async_computation | async-start | bytes 1310720 | tf_op jit(solution)/shard_map/all_to_all | solution.py:124
  16.2 52.2 %all-reduce.3.cloned.1.call-start = ((), (), s32[]{:S(2)}) async-start(), calls=%async_computation.1 | async-start | bytes 524288 | tf_op jit(solution)/shard_map/psum | solution.py:133
  16.4 8.7 copy-start.3
  37.0 104.8 %all-reduce.5.cloned.1.call-start = ((), (), s32[]{:S(2)}) async-start(), calls=%async_computation.2 | async-start | bytes 327680 | tf_op jit(solution)/shard_map/psum | solution.py:152
Sparse Core Ops, SparseCore 0:
  37.1 31.3 all-reduce.2
  71.8 69.9 all-reduce.4
where the time goes:
time: 1460 us; the launch traced here: 1440 us
  loops' own time  810 us (55%)
  other arithmetic  372 us (25%)
  waiting for transfers between devices  104 us (7%)
  matrix products  88.7 us (6%)
  local copies, waits for them, and re-layouts  48.2 us (3%)
    another operation x4, loops' own time, run_batch(): lax.fori_loop(0, count_blocks, one_block, (transforms, offsets, jnp.zeros...  810 us
    reduce_sum x248, other arithmetic, serial_block(): center_col = jnp.mean(column)  154 us
    reduce_sum x248, other arithmetic, serial_block(): jnp.sum(anomaly_col * anomaly_col) / denominator + errors[column_id]  153 us
    psum x1, waiting for transfers between devices, body(): bases = lax.psum(chosen, 'region')  66.7 us
    dot_general x248, matrix products, serial_block(): jnp.dot(anomaly_col, anomaly_all, precision=highest) / denominator  49.4 us
    reduce_sum x240, other arithmetic, serial_block(): anomaly_all = current - jnp.mean(current, axis=0, keepdims=True)  43.3 us
    psum x1, waiting for transfers between devices, body(): priors = lax.psum(partial_priors, 'lev')  31.1 us
  transfers between devices with their start and end apart: 3, of which 3 were waited for; matrix products, arithmetic and copies ran while one was open for 1% of the time, Pallas kernels for 0%

commit v1 on v0

v1 whole, which is shorter than its diff:
```python
import functools

import jax
import jax.numpy as jnp
from jax import lax
from jax.experimental import pallas as pl
from jax.experimental.pallas import tpu as pltpu
from jax.sharding import PartitionSpec as P

TILE = 32
STRIDE = 4
LANES = 128
SUB = 8

highest = lax.Precision.HIGHEST
f32 = jnp.float32
bf16 = jnp.bfloat16


def dot(a, b, ca, cb, precision=highest):
    return lax.dot_general(
        a, b, (((ca,), (cb,)), ((), ())), precision=precision, preferred_element_type=f32
    )


def iota(shape, dim):
    return lax.broadcasted_iota(jnp.int32, shape, dim)


def split3(x):
    hi = x.astype(bf16)
    rest = x - hi.astype(f32)
    mid = rest.astype(bf16)
    low = (rest - mid.astype(f32)).astype(bf16)
    return hi, mid, low


def prior_kernel(
    first_ref, down_ref, across_ref, home_ref, state_ref, kernel_ref, order_ref, table_ref,
    prior_ref, aux_ref,
):
    members, levels, regions, pixels = state_ref.shape
    count = order_ref.shape[1]
    batches = home_ref.shape[0]
    size = count // batches
    channels = kernel_ref.shape[0]
    sites = (TILE // STRIDE) * (TILE // STRIDE)

    lane = iota((1, count), 1)
    spread = jnp.where(
        iota((batches, count), 1) // size == iota((batches, count), 0), 1.0, 0.0
    ).astype(f32)
    hit = order_ref[...] == iota((size, count), 0)
    rows = []
    for name in range(3):
        wide = dot(table_ref[name], spread, 0, 0)
        rows.append(jnp.sum(jnp.where(hit, wide, 0.0), axis=0, keepdims=True))
    aux_ref[...] = jnp.concatenate(rows + [jnp.zeros((SUB - 3, count), f32)], axis=0)

    picked = rows[0].astype(jnp.int32)
    channel = picked // sites
    spot = picked - channel * sites
    spot_row = spot // (TILE // STRIDE)
    spot_col = spot - spot_row * (TILE // STRIDE)

    pixel = iota((pixels, 1), 0) + first_ref[0]
    row = pixel // TILE
    col = pixel - row * TILE
    weight_row = jnp.zeros((pixels, 1), f32)
    weight_col = jnp.zeros((pixels, 1), f32)
    for i in range(STRIDE):
        weight_row = jnp.where(row % STRIDE == i, down_ref[i], weight_row)
        weight_col = jnp.where(col % STRIDE == i, across_ref[i], weight_col)
    weight = weight_row * weight_col
    inside = (row // STRIDE == spot_row) & (col // STRIDE == spot_col)
    place = jnp.where(inside, weight, 0.0)

    total = jnp.zeros((members * regions, count), f32)
    for level in range(levels):
        height = jnp.zeros((1, count), f32)
        for c in range(channels):
            height = jnp.where(channel == c, kernel_ref[c, level], height)
        grid = state_ref[:, level].astype(f32).reshape(members * regions, pixels).astype(bf16)
        for piece in split3(place * height):
            total = total + dot(grid, piece, 1, 0, None)
    home = jnp.zeros((1, count), jnp.int32)
    for k in range(batches):
        home = jnp.where(lane // size == k, home_ref[k], home)
    here = iota((regions, count), 0) == home
    chosen = jnp.where(here[None], total.reshape(members, regions, count), 0.0)
    prior_ref[:members] = jnp.sum(chosen, axis=1)
    if prior_ref.shape[0] > members:
        prior_ref[members:] = jnp.zeros((prior_ref.shape[0] - members, count), f32)


def rep(x):
    return jnp.broadcast_to(x, (SUB, x.shape[1]))


def col(x, j):
    return jnp.broadcast_to(x[:, j : j + 1], (SUB, LANES))


def filter_kernel(members, own_ref, home_ref, radius_ref, base_ref, aux_ref, high_ref, low_ref, x_ref, h_ref, b_ref):
    padded, count = base_ref.shape
    batches = home_ref.shape[0]
    size = count // batches
    groups = size // SUB
    channels = radius_ref.shape[0]
    sites = (TILE // STRIDE) * (TILE // STRIDE)
    dof = members - 1.0
    E = padded
    lane = iota((1, LANES), 1)
    member = lane < members

    base = base_ref[...]
    if padded < LANES:
        base = jnp.concatenate([base, jnp.zeros((LANES - padded, count), f32)], axis=0)
    cols = base.T
    aux = aux_ref[...]
    aux_cols = jnp.concatenate([aux, jnp.zeros((LANES - SUB, count), f32)], axis=0).T
    center = jnp.sum(jnp.where(member, cols, 0.0), axis=1, keepdims=True) / members
    x_ref[:count] = jnp.where(
        lane == E, center - aux_cols[:, 1:2], jnp.where(member, cols - center, 0.0)
    )
    square = iota((LANES, LANES), 0)
    x_ref[count:] = jnp.where((square == iota((LANES, LANES), 1)) & (square < members), 1.0, 0.0)

    place = aux_cols[:, 0:1].astype(jnp.int32) // sites
    cut = jnp.zeros((count, 1), f32)
    for c in range(channels):
        cut = jnp.where(place == c, radius_ref[c].astype(f32), cut)
    inverse_cut = 1.0 / (cut + 1.0)
    noise = aux_cols[:, 2:3] * dof

    wide = count + LANES
    owner = jnp.zeros((1, wide), jnp.int32) + own_ref[0]
    for k in range(batches):
        owner = jnp.where(iota((1, wide), 1) // size == k, home_ref[k], owner)

    for b in range(batches):
        r0 = b * size
        xb = x_ref[r0 : r0 + size]
        xm = jnp.where(member, xb, 0.0)
        gram = dot(xm, xm, 1, 1)
        noise_b = noise[r0 : r0 + size]
        gram = gram + jnp.where(iota((size, size), 0) == iota((size, size), 1), noise_b, 0.0)
        G = [gram[SUB * g : SUB * g + SUB] for g in range(groups)]
        X = [xb[SUB * g : SUB * g + SUB] for g in range(groups)]
        for p in range(groups):
            C = [[col(G[g], SUB * p + j) for g in range(p, groups)] for j in range(SUB)]
            s = [[rep(C[j][0][i : i + 1]) for j in range(i + 1)] for i in range(SUB)]
            noise_p = jnp.broadcast_to(noise_b[SUB * p : SUB * p + SUB], (SUB, LANES))
            l = [[None] * SUB for _ in range(SUB)]
            inv = []
            for j in range(SUB):
                inv.append(1.0 / s[j][j])
                for i in range(j + 1, SUB):
                    l[i][j] = s[i][j] * inv[j]
                for i in range(j + 1, SUB):
                    for k in range(j + 1, i + 1):
                        s[i][k] = s[i][k] - l[i][j] * s[k][j]
            U, H, alpha = [], [], []
            for j in range(SUB):
                inv_alpha = 1.0 + jnp.sqrt(rep(noise_p[j : j + 1]) * inv[j])
                alpha.append(1.0 / inv_alpha)
                u = rep(G[p][j : j + 1])
                h = rep(X[p][j : j + 1])
                for i in range(j):
                    u = u - l[j][i][:, :size] * U[i]
                    h = h - (l[j][i] * alpha[i]) * H[i]
                h = jnp.where(lane == E, h * inv_alpha, h)
                U.append(u)
                H.append(h)
                row = jnp.where(lane == E + 1, alpha[j] * inv[j], h)
                h_ref[SUB * p + j : SUB * p + j + 1] = row[:1]
            for g in range(p + 1, groups):
                L = []
                for j in range(SUB):
                    c = C[j][g - p]
                    for i in range(j):
                        c = c - L[i] * s[j][i]
                    L.append(c * inv[j])
                for j in range(SUB):
                    G[g] = G[g] - L[j][:, :size] * U[j]
                    X[g] = X[g] - (L[j] * alpha[j]) * H[j]

        low = min((r0 + size) // LANES * LANES, count)
        span = wide - low
        hb = h_ref[...]
        hm = jnp.where(member, hb, 0.0)
        overlap = dot(hm, hm, 1, 1)
        xr = x_ref[low:]
        W = dot(hm, xr, 1, 1)
        far = jnp.abs(owner[:, low:] - home_ref[b]).astype(f32)
        taper = jnp.maximum(0.0, 1.0 - far * inverse_cut[r0 : r0 + size]) * hb[:, E + 1 : E + 2]
        S = [overlap[SUB * g : SUB * g + SUB] for g in range(groups)]
        W = [W[SUB * g : SUB * g + SUB] for g in range(groups)]
        tiles = span // LANES

        def scale(c, row):
            return jnp.concatenate(
                [c * row[:, LANES * t : LANES * t + LANES] for t in range(tiles)], axis=1
            )

        for p in range(groups):
            C = [[col(S[g], SUB * p + j) for g in range(p, groups)] for j in range(SUB)]
            B = []
            for j in range(SUB):
                w = rep(W[p][j : j + 1])
                for i in range(j):
                    w = w - scale(rep(C[i][0][j : j + 1]), B[i])
                beta = w * rep(taper[SUB * p + j : SUB * p + j + 1])
                B.append(beta)
                b_ref[SUB * p + j : SUB * p + j + 1, low:] = beta[:1]
            for g in range(p + 1, groups):
                for j in range(SUB):
                    W[g] = W[g] - scale(C[j][g - p], B[j])
        x_ref[low:] = xr - dot(b_ref[:, low:], hb, 0, 0)

    last = x_ref[count : count + members]
    mixing = jnp.where(member, last + last[:, E : E + 1], 0.0)
    mixing = mixing - jnp.sum(mixing, axis=0, keepdims=True) / members + 1.0 / members
    high = mixing.astype(bf16)
    high_ref[...] = high
    low_ref[...] = (mixing - high.astype(f32)).astype(bf16)


def swap(x, axis, n, k):
    return lax.ppermute(x, axis, [(i, i ^ k) for i in range(n)])


def reduce_over(x, axis, n):
    if n & (n - 1):
        return lax.psum(x, axis)
    stride = 1
    while stride < n:
        radix = 2 if (n // stride).bit_length() % 2 == 0 else 4
        x = x + sum(swap(x, axis, n, k * stride) for k in range(1, radix))
        stride *= radix
    return x


def total_over(x, region_count, level_count):
    rows, count = x.shape
    if level_count & (level_count - 1):
        return lax.psum(x, ("region", "lev"))
    me = lax.axis_index("lev")
    parts = x.reshape(level_count, rows // level_count, count)
    own = lax.dynamic_index_in_dim(parts, me, 0, keepdims=False)
    for k in range(1, level_count):
        piece = lax.dynamic_index_in_dim(parts, me ^ k, 0, keepdims=False)
        own = own + swap(piece, "lev", level_count, k)
    own = reduce_over(own, "region", region_count)
    held = jnp.stack([own] + [swap(own, "lev", level_count, k) for k in range(1, level_count)])
    return jnp.concatenate(
        [lax.dynamic_index_in_dim(held, me ^ v, 0, keepdims=False) for v in range(level_count)]
    )


def body(
    region_count,
    level_count,
    background_members,
    channel_height_kernel,
    sensor_spread_down,
    sensor_spread_across,
    measurement_placement,
    measurement_ordering,
    group_area_number,
    taper_radius_limit,
    measured_amounts,
    measurement_noise_spread,
):
    members, levels, pixels, regions = background_members.shape
    batches, size = measurement_ordering.shape
    count = batches * size
    own_region = lax.axis_index("region").astype(jnp.int32)

    state = jnp.transpose(background_members, (0, 1, 3, 2))
    if regions > 8:
        local = jnp.take(state, group_area_number, axis=2)
        home = jnp.arange(batches, dtype=jnp.int32)
    else:
        local, home = state, group_area_number
    table = jnp.stack(
        [measurement_placement.astype(f32), measured_amounts, measurement_noise_spread]
    )
    granule = SUB * level_count
    padded = -(-members // granule) * granule
    vmem = pl.BlockSpec(memory_space=pltpu.VMEM)
    smem = pl.BlockSpec(memory_space=pltpu.SMEM)
    partial, aux = pl.pallas_call(
        prior_kernel,
        out_shape=(
            jax.ShapeDtypeStruct((padded, count), f32),
            jax.ShapeDtypeStruct((SUB, count), f32),
        ),
        in_specs=[smem, smem, smem, smem, vmem, smem, vmem, vmem],
        out_specs=(vmem, vmem),
    )(
        (own_region * pixels)[None],
        sensor_spread_down,
        sensor_spread_across,
        home,
        local,
        channel_height_kernel,
        measurement_ordering.reshape(1, count),
        table,
    )
    base = total_over(partial, region_count, level_count)
    base, state = lax.optimization_barrier((base, state))
    pieces = pl.pallas_call(
        functools.partial(filter_kernel, members),
        out_shape=[jax.ShapeDtypeStruct((members, LANES), bf16)] * 2,
        in_specs=[smem, smem, smem, vmem, vmem],
        out_specs=[vmem, vmem],
        scratch_shapes=[
            pltpu.VMEM((count + LANES, LANES), f32),
            pltpu.VMEM((size, LANES), f32),
            pltpu.VMEM((size, count + LANES), f32),
        ],
        cost_estimate=pl.CostEstimate(flops=10**9, bytes_accessed=10**6, transcendentals=0),
    )(own_region[None], group_area_number, taper_radius_limit, base, aux)

    whole = lax.all_to_all(
        jnp.transpose(state, (2, 1, 0, 3)), "region", split_axis=0, concat_axis=0, tiled=True
    )
    field = jnp.transpose(whole, (2, 1, 0, 3)).reshape(members, -1)
    result = sum(dot(piece[:, :members], field, 0, 0, None) for piece in pieces)
    return result.reshape(members, levels, 1, pixels * region_count).astype(bf16)


def solution(mesh):
    return jax.shard_map(
        functools.partial(body, mesh.shape["region"], mesh.shape["lev"]),
        mesh=mesh,
        in_specs=(
            P(None, "lev", "region", None),
            P(None, "lev"),
            P(),
            P(),
            P(),
            P(),
            P(),
            P(),
            P(),
            P(),
        ),
        out_specs=P(None, "lev", "region", None),
        check_vma=False,
    )
```

time: 1460 us -> 59.5 us (0.04); the launches traced: 1440 us -> 59 us
  loops' own time: 810 us -> 0 us
  other arithmetic: 372 us -> 3.4 us
  waiting for transfers between devices: 104 us -> 12.8 us
  matrix products: 88.7 us -> 0.75 us
  local copies, waits for them, and re-layouts: 48.2 us -> 7.07 us
  Pallas kernels: 0 us -> 19.7 us
    another operation x4 -> x0, loops' own time: 810 us -> none  [run_batch(): lax.fori_loop(0, count_blocks, one_block, (transforms, offsets, jnp.zeros...]
    reduce_sum x755 -> x0, other arithmetic: 354 us -> none  [the longest x248 154 us: serial_block(): center_col = jnp.mean(column)]
    psum x2 -> x0, waiting for transfers between devices: 97.8 us -> none  [the longest x1 66.7 us: body(): bases = lax.psum(chosen, 'region')]
    dot_general x386 -> x2, matrix products: 88.7 us -> 0.75 us  [dot(): lax.dot_general(a, b, (((ca,), (cb,)), ((), ())), precision=precision, pr...]
    slice x42 -> x0, local copies, waits for them, and re-layouts: 28.3 us -> none  [the longest x16 11.4 us: serial_block(): innovation = values[column_id] - center_col]
    pallas_call x0 -> x2, Pallas kernels: none -> 19.7 us  [the longest x1 16.2 us: body(): pl.pallas_call(functools.partial(filter_kernel, members), out_shape=[jax....]
  transfers between devices with their start and end apart: 3 -> 11, of which waited for: 3 -> 8; matrix products, arithmetic and copies ran while one was open for 1% -> 0% of each run, Pallas kernels for 0% -> 27%
where the time goes in v1:
time: 59.5 us; the launch traced here: 59 us
  Pallas kernels  19.7 us (33%)
  starting transfers between devices  15.2 us (26%)
  waiting for transfers between devices  12.8 us (22%)
  local copies, waits for them, and re-layouts  7.07 us (12%)
  other arithmetic  3.4 us (6%)
  matrix products  0.75 us (1%)
    pallas_call x1, Pallas kernels, body(): pl.pallas_call(functools.partial(filter_kernel, members), out_shape=[jax....  16.2 us
    ppermute x10, waiting for transfers between devices, swap(): return lax.ppermute(x, axis, [(i, i ^ k) for i in range(n)])  12.1 us
    ppermute x10, starting transfers between devices, swap(): return lax.ppermute(x, axis, [(i, i ^ k) for i in range(n)])  10.9 us
    all_to_all x1, starting transfers between devices, body(): lax.all_to_all(jnp.transpose(state, (2, 1, 0, 3)), 'region', split_axis=0...  4.26 us
    pallas_call x1, Pallas kernels, body(): pl.pallas_call(prior_kernel, out_shape=(jax.ShapeDtypeStruct((padded, cou...  3.52 us
    another operation x2, other arithmetic, body(): jnp.stack([measurement_placement.astype(f32), measured_amounts, measureme...  1.98 us
    unnamed x7, local copies, waits for them, and re-layouts  1.68 us
    reshape x1, local copies, waits for them, and re-layouts, body(): measurement_ordering.reshape(1, count)  1.42 us
  transfers between devices with their start and end apart: 11, of which 8 were waited for; matrix products, arithmetic and copies ran while one was open for 0% of the time, Pallas kernels for 27%

profile of v1, /device:TPU:0, one launch (start us, length us, event | category | flops | bytes accessed | tf_op | source)
XLA Modules:
  0.0 59.0 jit_solution(3117194644450151705)
XLA Ops:
  0.0 0.0 copy-start
  0.0 1.4 %reshape.23.order_ref = s32[1,256]{1,0:T(1,128)} reshape(s32[4,64]{1,0:T(4,128)} %param.15) | data formatting | bytes 2048 | tf_op jit(solution)/shard_map/reshape | solution.py:308
  1.4 0.7 %convert_bitcast_fusion = f32[1,4,64]{2,1,0:T(4,128)S(1)} fusion(s32[4,64]{1,0:T(4,128)} %param.14), kind=kLoop, calls=%fused_computation.23 | loop fusion | flops 256 | bytes 2048 | tf_op jit(solution)/shard_map/stack | solution.py:286
  2.1 1.3 %copy.16.kernel_ref = f32[8,4]{1,0:T(8,128)} copy(f32[8,4]{0,1:T(4,128)} %param.11) | data formatting | bytes 256 | tf_op args[1]
  3.5 1.3 %pad_maximum_fusion.2.table_ref = f32[3,4,64]{2,1,0:T(4,128)} fusion(f32[1,4,64]{2,1,0:T(4,128)} %bitcast.53, f32[1,4,64]{2,1,0:T(4,128)} %bitcast.54, f32[1,4,64]{2,1,0:T(4,128)S(1)} %convert_bitcast_fusion), kind=kLoop, calls=%fused_computation.22 | loop fusion | flops 1536 | bytes 6144 | tf_op jit(solution)/shard_map/stack | solution.py:286
  4.7 3.5 %shard_map.100 = (f32[96,256]{1,0:T(8,128)}, f32[8,256]{1,0:T(8,128)}) custom-call(s32[1]{0:T(128)} %bitcast.1.first_ref, f32[4]{0:T(128)} %down_ref.1, f32[4]{0:T(128)} %across_ref.1, s32[4]{0:T(128)} %home_ref.3, bf16[80,4,8,128]{3,2,1,0:T(8,128)(2,1)} %bitcast.44, f32[8,4]{1,0:T(8,128)} %copy.16.kernel_ref, s32[1,256]{1,0:T(1,128)} %reshape.23.order_ref, ...), custom_call_target="tpu_custom_call" | custom-call | tf_op jit(solution)/shard_map/pallas_call | solution.py:293
  8.3 0.8 %dynamic-slice_bitcast_fusion.6 = (f32[24,256]{1,0:T(8,128)S(1)}, f32[24,256]{1,0:T(8,128)S(1)}, f32[24,256]{1,0:T(8,128)S(1)}) fusion(f32[4,24,256]{2,1,0:T(8,128)} %bitcast.47, s32[]{:T(128)S(6)} %select_n.18, s32[]{:T(128)S(6)} %select_n.20, s32[]{:T(128)S(6)} %select_n.19), kind=kLoop, calls=%fused_computation.19 | loop fusion | bytes 147468 | tf_op jit(solution)/shard_map/jit(dynamic_index_in_dim)/squeeze | solution.py:252
  9.0 0.5 collective-permute-start
  9.5 2.6 %collective-permute-start.2 = (f32[24,256]{1,0:T(8,128)S(1)}, f32[24,256]{1,0:T(8,128)S(1)}, u32[]{:S(2)}, u32[]{:S(2)}) collective-permute-start(f32[24,256]{1,0:T(8,128)S(1)} %get-tuple-element.22), channel_id=1, source_target_pairs={{0,3},{1,2},{2,1},{3,0},{4,7},{5,6},{6,5},{7,4},{8,11},{9,10},{10,... | collective-permute-start | bytes 73736 | tf_op jit(solution)/shard_map/ppermute | solution.py:230
  12.1 0.0 collective-permute-start.1
  12.2 0.0 collective-permute-done
  12.2 1.5 %collective-permute-done.2 = f32[24,256]{1,0:T(8,128)S(1)} collective-permute-done((f32[24,256]{1,0:T(8,128)S(1)}, f32[24,256]{1,0:T(8,128)S(1)}, u32[]{:S(2)}, u32[]{:S(2)}) %collective-permute-start.2) | collective-permute-done | bytes 24608 | tf_op jit(solution)/shard_map/ppermute | solution.py:230
  13.6 2.3 %collective-permute-done.1 = f32[24,256]{1,0:T(8,128)S(1)} collective-permute-done((f32[24,256]{1,0:T(8,128)S(1)}, f32[24,256]{1,0:T(8,128)S(1)}, u32[]{:S(2)}, u32[]{:S(2)}) %collective-permute-start.1) | collective-permute-done | bytes 24608 | tf_op jit(solution)/shard_map/ppermute | solution.py:230
  16.0 0.7 %fusion.7 = f32[24,256]{1,0:T(8,128)S(1)} fusion(f32[24,256]{1,0:T(8,128)S(1)} %collective-permute-done.2, f32[24,256]{1,0:T(8,128)S(1)} %collective-permute-done.1, f32[24,256]{1,0:T(8,128)S(1)} %collective-permute-done, f32[4,24,256]{2,1,0:T(8,128)} %bitcast.48, s32[]{:T(128)S(6)} %select_n.17), kind=kLoop, calls=%fused_computation.11 | loop fusion | flops 18432 | bytes 122884 | tf_op jit(solution)/shard_map/add | solution.py:253
  16.7 1.5 %collective-permute-start.3 = (f32[24,256]{1,0:T(8,128)S(1)}, f32[24,256]{1,0:T(8,128)S(1)}, u32[]{:S(2)}, u32[]{:S(2)}) collective-permute-start(f32[24,256]{1,0:T(8,128)S(1)} %fusion.7), channel_id=1, source_target_pairs={{0,4},{4,0},{8,12},{12,8},{16,20},{20,16},{24,28},{28,24},{1,5},{5... | collective-permute-start | bytes 73736 | tf_op jit(solution)/shard_map/ppermute | solution.py:230
  18.2 2.3 %collective-permute-done.3 = f32[24,256]{1,0:T(8,128)S(1)} collective-permute-done((f32[24,256]{1,0:T(8,128)S(1)}, f32[24,256]{1,0:T(8,128)S(1)}, u32[]{:S(2)}, u32[]{:S(2)}) %collective-permute-start.3) | collective-permute-done | bytes 24608 | tf_op jit(solution)/shard_map/ppermute | solution.py:230
  20.5 3.6 %collective-permute-start.6 = (f32[24,256]{1,0:T(8,128)S(1)}, f32[24,256]{1,0:T(8,128)S(1)}, u32[]{:S(2)}, u32[]{:S(2)}) collective-permute-start(f32[24,256]{1,0:T(8,128)S(1)} %add.48), channel_id=1, source_target_pairs={{0,24},{4,28},{8,16},{12,20},{16,8},{20,12},{24,0},{28,4},{1,25},{... | collective-permute-start | bytes 73736 | tf_op jit(solution)/shard_map/ppermute | solution.py:230
  24.1 0.0 collective-permute-start.5
  24.1 0.8 %collective-permute-start.4 = (f32[24,256]{1,0:T(8,128)S(1)}, f32[24,256]{1,0:T(8,128)S(1)}, u32[]{:S(2)}, u32[]{:S(2)}) collective-permute-start(f32[24,256]{1,0:T(8,128)S(1)} %add.48), channel_id=1, source_target_pairs={{0,8},{4,12},{8,0},{12,4},{16,24},{20,28},{24,16},{28,20},{1,9},{5... | collective-permute-start | bytes 73736 | tf_op jit(solution)/shard_map/ppermute | solution.py:230
  24.9 1.2 %collective-permute-done.6 = f32[24,256]{1,0:T(8,128)S(1)} collective-permute-done((f32[24,256]{1,0:T(8,128)S(1)}, f32[24,256]{1,0:T(8,128)S(1)}, u32[]{:S(2)}, u32[]{:S(2)}) %collective-permute-start.6) | collective-permute-done | bytes 24608 | tf_op jit(solution)/shard_map/ppermute | solution.py:230
  26.2 2.7 %collective-permute-done.5 = f32[24,256]{1,0:T(8,128)S(1)} collective-permute-done((f32[24,256]{1,0:T(8,128)S(1)}, f32[24,256]{1,0:T(8,128)S(1)}, u32[]{:S(2)}, u32[]{:S(2)}) %collective-permute-start.5) | collective-permute-done | bytes 24608 | tf_op jit(solution)/shard_map/ppermute | solution.py:230
  28.9 0.0 collective-permute-done.4
  28.9 0.1 collective-permute-start.9
  29.0 0.6 %collective-permute-start.8 = (f32[24,256]{1,0:T(8,128)S(1)}, f32[24,256]{1,0:T(8,128)S(1)}, u32[]{:S(2)}, u32[]{:S(2)}) collective-permute-start(f32[24,256]{1,0:T(8,128)S(1)} %add_add_fusion), channel_id=1, source_target_pairs={{0,2},{1,3},{2,0},{3,1},{4,6},{5,7},{6,4},{7,5},{8,10},{9,11},{10,... | collective-permute-start | bytes 73736 | tf_op jit(solution)/shard_map/ppermute | solution.py:230
  29.6 1.2 %collective-permute-start.7 = (f32[24,256]{1,0:T(8,128)S(1)}, f32[24,256]{1,0:T(8,128)S(1)}, u32[]{:S(2)}, u32[]{:S(2)}) collective-permute-start(f32[24,256]{1,0:T(8,128)S(1)} %add_add_fusion), channel_id=1, source_target_pairs={{0,1},{1,0},{2,3},{3,2},{4,5},{5,4},{6,7},{7,6},{8,9},{9,8},{10,11... | collective-permute-start | bytes 73736 | tf_op jit(solution)/shard_map/ppermute | solution.py:230
  30.8 1.4 %collective-permute-done.9 = f32[24,256]{1,0:T(8,128)S(1)} collective-permute-done((f32[24,256]{1,0:T(8,128)S(1)}, f32[24,256]{1,0:T(8,128)S(1)}, u32[]{:S(2)}, u32[]{:S(2)}) %collective-permute-start.9) | collective-permute-done | bytes 24608 | tf_op jit(solution)/shard_map/ppermute | solution.py:230
  32.2 0.7 %collective-permute-done.8 = f32[24,256]{1,0:T(8,128)S(1)} collective-permute-done((f32[24,256]{1,0:T(8,128)S(1)}, f32[24,256]{1,0:T(8,128)S(1)}, u32[]{:S(2)}, u32[]{:S(2)}) %collective-permute-start.8) | collective-permute-done | bytes 24608 | tf_op jit(solution)/shard_map/ppermute | solution.py:230
  32.8 0.0 collective-permute-done.7
  32.9 0.7 %pad_maximum_fusion.1.base_ref = f32[96,256]{1,0:T(8,128)} fusion(f32[24,256]{1,0:T(8,128)S(1)} %get-tuple-element.18, f32[24,256]{1,0:T(8,128)S(1)} %get-tuple-element.19, f32[24,256]{1,0:T(8,128)S(1)} %get-tuple-element.20, f32[24,256]{1,0:T(8,128)S(1)} %get-tuple-element.17), kind=kLoop, calls=%fused_computation.8 | loop fusion | flops 73728 | bytes 196608 | tf_op jit(solution)/shard_map/concatenate | solution.py:256
  33.5 0.0 copy-done
  33.5 1.1 %copy.17 = bf16[8,4,80,128]{3,1,2,0:T(4,128)(2,1)} copy(bf16[8,4,80,128]{3,0,1,2:T(8,128)(2,1)S(1)} %bitcast.45) | data formatting | bytes 1310720 | tf_op jit(solution)/shard_map/transpose | solution.py:327
  34.6 4.3 %all-to-all-start = ((bf16[8,4,80,128]{3,1,2,0:T(4,128)(2,1)}), bf16[8,4,80,128]{3,1,2,0:T(4,128)(2,1)S(1)}, u32[]{:S(2)}, u32[]{:S(2)}) async-start(bf16[8,4,80,128]{3,1,2,0:T(4,128)(2,1)} %copy.17), calls=%async_computation | async-start | bytes 1310720 | tf_op jit(solution)/shard_map/all_to_all | solution.py:326
  38.9 16.2 %shard_map.101 = (bf16[80,128]{1,0:T(8,128)(2,1)}, bf16[80,128]{1,0:T(8,128)(2,1)}) custom-call(s32[1]{0:T(128)} %bitcast.own_ref, s32[4]{0:T(128)} %home_ref.3, s32[8]{0:T(128)} %radius_ref.1, f32[96,256]{1,0:T(8,128)} %pad_maximum_fusion.1.base_ref, f32[8,256]{1,0:T(8,128)} %get-tuple-element.13.aux_ref), custom_call_target="tpu_custom_call" | custom-call | flops 1000000000 | bytes 1000000 | tf_op jit(solution)/shard_map/pallas_call | solution.py:313
  55.1 0.0 copy-start.2
  55.1 0.7 %all-to-all-done = bf16[8,4,80,128]{3,1,2,0:T(4,128)(2,1)S(1)} async-done(((bf16[8,4,80,128]{3,1,2,0:T(4,128)(2,1)}), bf16[8,4,80,128]{3,1,2,0:T(4,128)(2,1)S(1)}, u32[]{:S(2)}, u32[]{:S(2)}) %all-to-all-start) | async-done | bytes 655392 | tf_op jit(solution)/shard_map/all_to_all | solution.py:326
  55.8 0.8 %copy.18 = bf16[80,4,8,128]{3,2,1,0:T(8,128)(2,1)S(1)} copy(bf16[80,4,8,128]{3,1,0,2:T(4,128)(2,1)S(1)} %bitcast.46) | data formatting | bytes 1310720 | tf_op jit(solution)/shard_map/transpose | solution.py:329
  56.6 0.0 copy-start.1
  56.6 0.0 copy-done.2
  56.6 0.4 fusion.2
  57.0 0.3 copy-done.1
  57.3 0.4 fusion
  57.7 1.3 %convert_element_type.19 = bf16[80,4,1,1024]{3,1,0,2:T(4,128)(2,1)} reshape(bf16[80,4096]{1,0:T(8,128)(2,1)S(1)} %fusion) | data formatting | bytes 1310720 | tf_op jit(solution)/shard_map/convert_element_type | solution.py:331
  (4 shorter events, 0.0 us)
Async XLA Ops:
  0.0 33.5 %copy-start = (bf16[80,4,128,8]{2,3,1,0:T(8,128)(2,1)S(1)}, bf16[80,4,128,8]{2,3,1,0:T(8,128)(2,1)}, u32[]{:S(2)}) copy-start(bf16[80,4,128,8]{2,3,1,0:T(8,128)(2,1)} %param.10) | copy-start | bytes 1966084
  9.0 3.1 %collective-permute-start = (f32[24,256]{1,0:T(8,128)S(1)}, f32[24,256]{1,0:T(8,128)S(1)}, u32[]{:S(2)}, u32[]{:S(2)}) collective-permute-start(f32[24,256]{1,0:T(8,128)S(1)} %get-tuple-element.21), channel_id=1, source_target_pairs={{0,1},{1,0},{2,3},{3,2},{4,5},{5,4},{6,7},{7,6},{8,9},{9,8},{10,11... | collective-permute-start | bytes 73736 | tf_op jit(solution)/shard_map/ppermute | solution.py:230
  9.5 4.1 %collective-permute-start.2 = (f32[24,256]{1,0:T(8,128)S(1)}, f32[24,256]{1,0:T(8,128)S(1)}, u32[]{:S(2)}, u32[]{:S(2)}) collective-permute-start(f32[24,256]{1,0:T(8,128)S(1)} %get-tuple-element.22), channel_id=1, source_target_pairs={{0,3},{1,2},{2,1},{3,0},{4,7},{5,6},{6,5},{7,4},{8,11},{9,10},{10,... | collective-permute-start | bytes 73736 | tf_op jit(solution)/shard_map/ppermute | solution.py:230
  12.1 3.8 %collective-permute-start.1 = (f32[24,256]{1,0:T(8,128)S(1)}, f32[24,256]{1,0:T(8,128)S(1)}, u32[]{:S(2)}, u32[]{:S(2)}) collective-permute-start(f32[24,256]{1,0:T(8,128)S(1)} %get-tuple-element.23), channel_id=1, source_target_pairs={{0,2},{1,3},{2,0},{3,1},{4,6},{5,7},{6,4},{7,5},{8,10},{9,11},{10,... | collective-permute-start | bytes 73736 | tf_op jit(solution)/shard_map/ppermute | solution.py:230
  16.7 3.8 %collective-permute-start.3 = (f32[24,256]{1,0:T(8,128)S(1)}, f32[24,256]{1,0:T(8,128)S(1)}, u32[]{:S(2)}, u32[]{:S(2)}) collective-permute-start(f32[24,256]{1,0:T(8,128)S(1)} %fusion.7), channel_id=1, source_target_pairs={{0,4},{4,0},{8,12},{12,8},{16,20},{20,16},{24,28},{28,24},{1,5},{5... | collective-permute-start | bytes 73736 | tf_op jit(solution)/shard_map/ppermute | solution.py:230
  20.5 5.6 %collective-permute-start.6 = (f32[24,256]{1,0:T(8,128)S(1)}, f32[24,256]{1,0:T(8,128)S(1)}, u32[]{:S(2)}, u32[]{:S(2)}) collective-permute-start(f32[24,256]{1,0:T(8,128)S(1)} %add.48), channel_id=1, source_target_pairs={{0,24},{4,28},{8,16},{12,20},{16,8},{20,12},{24,0},{28,4},{1,25},{... | collective-permute-start | bytes 73736 | tf_op jit(solution)/shard_map/ppermute | solution.py:230
  24.1 4.7 %collective-permute-start.5 = (f32[24,256]{1,0:T(8,128)S(1)}, f32[24,256]{1,0:T(8,128)S(1)}, u32[]{:S(2)}, u32[]{:S(2)}) collective-permute-start(f32[24,256]{1,0:T(8,128)S(1)} %add.48), channel_id=1, source_target_pairs={{0,16},{4,20},{8,24},{12,28},{16,0},{20,4},{24,8},{28,12},{1,17},{... | collective-permute-start | bytes 73736 | tf_op jit(solution)/shard_map/ppermute | solution.py:230
  24.1 4.7 %collective-permute-start.4 = (f32[24,256]{1,0:T(8,128)S(1)}, f32[24,256]{1,0:T(8,128)S(1)}, u32[]{:S(2)}, u32[]{:S(2)}) collective-permute-start(f32[24,256]{1,0:T(8,128)S(1)} %add.48), channel_id=1, source_target_pairs={{0,8},{4,12},{8,0},{12,4},{16,24},{20,28},{24,16},{28,20},{1,9},{5... | collective-permute-start | bytes 73736 | tf_op jit(solution)/shard_map/ppermute | solution.py:230
  28.9 3.3 %collective-permute-start.9 = (f32[24,256]{1,0:T(8,128)S(1)}, f32[24,256]{1,0:T(8,128)S(1)}, u32[]{:S(2)}, u32[]{:S(2)}) collective-permute-start(f32[24,256]{1,0:T(8,128)S(1)} %add_add_fusion), channel_id=1, source_target_pairs={{0,3},{1,2},{2,1},{3,0},{4,7},{5,6},{6,5},{7,4},{8,11},{9,10},{10,... | collective-permute-start | bytes 73736 | tf_op jit(solution)/shard_map/ppermute | solution.py:230
  29.0 3.9 %collective-permute-start.8 = (f32[24,256]{1,0:T(8,128)S(1)}, f32[24,256]{1,0:T(8,128)S(1)}, u32[]{:S(2)}, u32[]{:S(2)}) collective-permute-start(f32[24,256]{1,0:T(8,128)S(1)} %add_add_fusion), channel_id=1, source_target_pairs={{0,2},{1,3},{2,0},{3,1},{4,6},{5,7},{6,4},{7,5},{8,10},{9,11},{10,... | collective-permute-start | bytes 73736 | tf_op jit(solution)/shard_map/ppermute | solution.py:230
  29.6 3.3 %collective-permute-start.7 = (f32[24,256]{1,0:T(8,128)S(1)}, f32[24,256]{1,0:T(8,128)S(1)}, u32[]{:S(2)}, u32[]{:S(2)}) collective-permute-start(f32[24,256]{1,0:T(8,128)S(1)} %add_add_fusion), channel_id=1, source_target_pairs={{0,1},{1,0},{2,3},{3,2},{4,5},{5,4},{6,7},{7,6},{8,9},{9,8},{10,11... | collective-permute-start | bytes 73736 | tf_op jit(solution)/shard_map/ppermute | solution.py:230
  34.6 21.2 %all-to-all-start = ((bf16[8,4,80,128]{3,1,2,0:T(4,128)(2,1)}), bf16[8,4,80,128]{3,1,2,0:T(4,128)(2,1)S(1)}, u32[]{:S(2)}, u32[]{:S(2)}) async-start(bf16[8,4,80,128]{3,1,2,0:T(4,128)(2,1)} %copy.17), calls=%async_computation | async-start | bytes 1310720 | tf_op jit(solution)/shard_map/all_to_all | solution.py:326
  55.1 1.5 %copy-start.2 = (bf16[80,128]{1,0:T(8,128)(2,1)S(1)}, bf16[80,128]{1,0:T(8,128)(2,1)}, u32[]{:S(2)}) copy-start(bf16[80,128]{1,0:T(8,128)(2,1)} %get-tuple-element.14) | copy-start | bytes 61444
  56.6 0.7 %copy-start.1 = (bf16[80,128]{1,0:T(8,128)(2,1)S(1)}, bf16[80,128]{1,0:T(8,128)(2,1)}, u32[]{:S(2)}) copy-start(bf16[80,128]{1,0:T(8,128)(2,1)} %get-tuple-element.16) | copy-start | bytes 61444

commit v2 on v1

--- a/solution.py
+++ b/solution.py
@@ -7,6 +7,7 @@
 from jax.experimental.pallas import tpu as pltpu
 from jax.sharding import PartitionSpec as P
 
+
 TILE = 32
 STRIDE = 4
 LANES = 128
@@ -35,25 +36,35 @@
     return hi, mid, low
 
 
-def prior_kernel(
-    first_ref, down_ref, across_ref, home_ref, state_ref, kernel_ref, order_ref, table_ref,
-    prior_ref, aux_ref,
-):
+def prior_kernel(first_ref, half_ref, *refs):
+    inputs, (keep_ref, send_ref, aux_ref), held, arrived = (
+        refs[:9], refs[9:12], refs[12:21], refs[21]
+    )
+    copies = [
+        pltpu.make_async_copy(source, target, arrived.at[i])
+        for i, (source, target) in enumerate(zip(inputs, held))
+    ]
+    for copy in copies:
+        copy.start()
+    for copy in copies[:-1]:
+        copy.wait()
+    (down_ref, across_ref, home_ref, height_ref, order_ref, place_ref, amount_ref, noise_ref,
+     state_ref) = held
     members, levels, regions, pixels = state_ref.shape
-    count = order_ref.shape[1]
-    batches = home_ref.shape[0]
-    size = count // batches
-    channels = kernel_ref.shape[0]
+    batches, size = order_ref.shape
+    count = batches * size
+    channels = height_ref.shape[1]
     sites = (TILE // STRIDE) * (TILE // STRIDE)
 
     lane = iota((1, count), 1)
     spread = jnp.where(
         iota((batches, count), 1) // size == iota((batches, count), 0), 1.0, 0.0
     ).astype(f32)
-    hit = order_ref[...] == iota((size, count), 0)
+    order = jnp.concatenate([order_ref[k : k + 1] for k in range(batches)], axis=1)
+    hit = order == iota((size, count), 0)
     rows = []
-    for name in range(3):
-        wide = dot(table_ref[name], spread, 0, 0)
+    for ref in (place_ref, amount_ref, noise_ref):
+        wide = dot(ref[...].astype(f32), spread, 0, 0)
         rows.append(jnp.sum(jnp.where(hit, wide, 0.0), axis=0, keepdims=True))
     aux_ref[...] = jnp.concatenate(rows + [jnp.zeros((SUB - 3, count), f32)], axis=0)
 
@@ -62,6 +73,8 @@
     spot = picked - channel * sites
     spot_row = spot // (TILE // STRIDE)
     spot_col = spot - spot_row * (TILE // STRIDE)
+    chosen = jnp.where(iota((channels, count), 0) == channel, 1.0, 0.0).astype(f32)
+    heights = dot(height_ref[...], chosen, 1, 0)
 
     pixel = iota((pixels, 1), 0) + first_ref[0]
     row = pixel // TILE
@@ -75,22 +88,23 @@
     inside = (row // STRIDE == spot_row) & (col // STRIDE == spot_col)
     place = jnp.where(inside, weight, 0.0)
 
+    copies[-1].wait()
     total = jnp.zeros((members * regions, count), f32)
     for level in range(levels):
-        height = jnp.zeros((1, count), f32)
-        for c in range(channels):
-            height = jnp.where(channel == c, kernel_ref[c, level], height)
         grid = state_ref[:, level].astype(f32).reshape(members * regions, pixels).astype(bf16)
-        for piece in split3(place * height):
+        for piece in split3(place * heights[level : level + 1]):
             total = total + dot(grid, piece, 1, 0, None)
     home = jnp.zeros((1, count), jnp.int32)
     for k in range(batches):
         home = jnp.where(lane // size == k, home_ref[k], home)
     here = iota((regions, count), 0) == home
-    chosen = jnp.where(here[None], total.reshape(members, regions, count), 0.0)
-    prior_ref[:members] = jnp.sum(chosen, axis=1)
-    if prior_ref.shape[0] > members:
-        prior_ref[members:] = jnp.zeros((prior_ref.shape[0] - members, count), f32)
+    share = jnp.sum(jnp.where(here[None], total.reshape(members, regions, count), 0.0), axis=1)
+    half = keep_ref.shape[0]
+    if 2 * half > members:
+        share = jnp.concatenate([share, jnp.zeros((2 * half - members, count), f32)], axis=0)
+    first = half_ref[0] == 0
+    keep_ref[...] = jnp.where(first, share[:half], share[half:])
+    send_ref[...] = jnp.where(first, share[half:], share[:half])
 
 
 def rep(x):
@@ -101,8 +115,11 @@
     return jnp.broadcast_to(x[:, j : j + 1], (SUB, LANES))
 
 
-def filter_kernel(members, own_ref, home_ref, radius_ref, base_ref, aux_ref, high_ref, low_ref, x_ref, h_ref, b_ref):
-    padded, count = base_ref.shape
+def filter_kernel(
+    members, own_ref, half_ref, home_ref, radius_ref, mine_ref, other_ref, aux_ref, high_ref, low_ref,
+    x_ref, h_ref, b_ref,
+):
+    padded, count = 2 * mine_ref.shape[0], mine_ref.shape[1]
     batches = home_ref.shape[0]
     size = count // batches
     groups = size // SUB
@@ -113,7 +130,11 @@
     lane = iota((1, LANES), 1)
     member = lane < members
 
-    base = base_ref[...]
+    first = half_ref[0] == 0
+    mine, other = mine_ref[...], other_ref[...]
+    base = jnp.concatenate(
+        [jnp.where(first, mine, other), jnp.where(first, other, mine)], axis=0
+    )
     if padded < LANES:
         base = jnp.concatenate([base, jnp.zeros((LANES - padded, count), f32)], axis=0)
     cols = base.T
@@ -226,36 +247,33 @@
     low_ref[...] = (mixing - high.astype(f32)).astype(bf16)
 
 
-def swap(x, axis, n, k):
-    return lax.ppermute(x, axis, [(i, i ^ k) for i in range(n)])
-
-
-def reduce_over(x, axis, n):
-    if n & (n - 1):
-        return lax.psum(x, axis)
-    stride = 1
-    while stride < n:
-        radix = 2 if (n // stride).bit_length() % 2 == 0 else 4
-        x = x + sum(swap(x, axis, n, k * stride) for k in range(1, radix))
-        stride *= radix
-    return x
-
-
-def total_over(x, region_count, level_count):
-    rows, count = x.shape
-    if level_count & (level_count - 1):
-        return lax.psum(x, ("region", "lev"))
-    me = lax.axis_index("lev")
-    parts = x.reshape(level_count, rows // level_count, count)
-    own = lax.dynamic_index_in_dim(parts, me, 0, keepdims=False)
-    for k in range(1, level_count):
-        piece = lax.dynamic_index_in_dim(parts, me ^ k, 0, keepdims=False)
-        own = own + swap(piece, "lev", level_count, k)
-    own = reduce_over(own, "region", region_count)
-    held = jnp.stack([own] + [swap(own, "lev", level_count, k) for k in range(1, level_count)])
-    return jnp.concatenate(
-        [lax.dynamic_index_in_dim(held, me ^ v, 0, keepdims=False) for v in range(level_count)]
-    )
+BOTH = ("region", "lev")
+
+
+def swap(x, devices, k):
+    return lax.ppermute(x, BOTH, [(i, i ^ k) for i in range(devices)])
+
+
+def exchange(keep, send, state, devices):
+    total = keep + swap(send, devices, 1)
+    bit = 2
+    while bit < devices:
+        last = 4 * bit >= devices
+        steps = (bit, 2 * bit, 3 * bit) if 2 * bit < devices else (bit,)
+        if bit == 2:
+            total, state = lax.optimization_barrier((total, state))
+            state = jnp.transpose(state, (2, 1, 0, 3))
+        if last:
+            total, state = lax.optimization_barrier((total, state))
+            moved = [swap(total, devices, k) for k in steps]
+            whole = lax.all_to_all(
+                state, "region", split_axis=0, concat_axis=0, tiled=True
+            )
+        else:
+            moved = [swap(total, devices, k) for k in steps]
+        total = total + sum(moved)
+        bit *= 4
+    return total, swap(total, devices, 1), whole
 
 
 def body(
@@ -283,49 +301,53 @@
         home = jnp.arange(batches, dtype=jnp.int32)
     else:
         local, home = state, group_area_number
-    table = jnp.stack(
-        [measurement_placement.astype(f32), measured_amounts, measurement_noise_spread]
-    )
-    granule = SUB * level_count
-    padded = -(-members // granule) * granule
+    half = -(-members // (2 * SUB)) * SUB
+    devices = region_count * level_count
+    side = ((own_region * level_count + lax.axis_index("lev")) % 2).astype(jnp.int32)[None]
     vmem = pl.BlockSpec(memory_space=pltpu.VMEM)
     smem = pl.BlockSpec(memory_space=pltpu.SMEM)
-    partial, aux = pl.pallas_call(
+    scalars = (sensor_spread_down, sensor_spread_across, home)
+    tables = (
+        jnp.transpose(channel_height_kernel),
+        measurement_ordering,
+        measurement_placement,
+        measured_amounts,
+        measurement_noise_spread,
+        local,
+    )
+    keep, send, aux = pl.pallas_call(
         prior_kernel,
         out_shape=(
-            jax.ShapeDtypeStruct((padded, count), f32),
+            jax.ShapeDtypeStruct((half, count), f32),
+            jax.ShapeDtypeStruct((half, count), f32),
             jax.ShapeDtypeStruct((SUB, count), f32),
         ),
-        in_specs=[smem, smem, smem, smem, vmem, smem, vmem, vmem],
-        out_specs=(vmem, vmem),
+        in_specs=[smem] * 2 + [pl.BlockSpec(memory_space=pltpu.HBM)] * 9,
+        out_specs=(vmem, vmem, vmem),
+        scratch_shapes=[pltpu.SMEM(x.shape, x.dtype) for x in scalars]
+        + [pltpu.VMEM(x.shape, x.dtype) for x in tables]
+        + [pltpu.SemaphoreType.DMA((9,))],
+        compiler_params=pltpu.CompilerParams(vmem_limit_bytes=24 * 2**20),
     )(
         (own_region * pixels)[None],
-        sensor_spread_down,
-        sensor_spread_across,
-        home,
-        local,
-        channel_height_kernel,
-        measurement_ordering.reshape(1, count),
-        table,
-    )
-    base = total_over(partial, region_count, level_count)
-    base, state = lax.optimization_barrier((base, state))
+        side,
+        *[pltpu.with_memory_space_constraint(x, pltpu.HBM) for x in (*scalars, *tables)],
+    )
+    mine, other, whole = exchange(keep, send, state, devices)
     pieces = pl.pallas_call(
         functools.partial(filter_kernel, members),
         out_shape=[jax.ShapeDtypeStruct((members, LANES), bf16)] * 2,
-        in_specs=[smem, smem, smem, vmem, vmem],
+        in_specs=[smem] * 4 + [vmem] * 3,
         out_specs=[vmem, vmem],
         scratch_shapes=[
             pltpu.VMEM((count + LANES, LANES), f32),
             pltpu.VMEM((size, LANES), f32),
             pltpu.VMEM((size, count + LANES), f32),
         ],
+        compiler_params=pltpu.CompilerParams(vmem_limit_bytes=16 * 2**20),
         cost_estimate=pl.CostEstimate(flops=10**9, bytes_accessed=10**6, transcendentals=0),
-    )(own_region[None], group_area_number, taper_radius_limit, base, aux)
-
-    whole = lax.all_to_all(
-        jnp.transpose(state, (2, 1, 0, 3)), "region", split_axis=0, concat_axis=0, tiled=True
-    )
+    )(own_region[None], side, group_area_number, taper_radius_limit, mine, other, aux)
+
     field = jnp.transpose(whole, (2, 1, 0, 3)).reshape(members, -1)
     result = sum(dot(piece[:, :members], field, 0, 0, None) for piece in pieces)
     return result.reshape(members, levels, 1, pixels * region_count).astype(bf16)

time: 59.5 us -> 58.7 us (0.987)
  waiting for transfers between devices: 12.8 us -> 21.2 us
  local copies, waits for them, and re-layouts: 7.07 us -> 3.18 us
  other arithmetic: 3.4 us -> 0.03 us
  Pallas kernels: 19.7 us -> 18 us
    ppermute x10 -> x8, waiting for transfers between devices: 12.1 us -> 21.1 us  [swap(): return lax.ppermute(x, BOTH, [(i, i ^ k) for i in range(devices)])]
    another operation x3 -> x0, other arithmetic: 1.98 us -> none  [the longest x2 1.98 us: body(): jnp.stack([measurement_placement.astype(f32), measured_amounts, measureme...]
    unnamed x7 -> x6, local copies, waits for them, and re-layouts: 1.68 us -> 0.02 us
    all_to_all x1, starting transfers between devices: 4.26 us -> 5.83 us  [exchange(): lax.all_to_all(state, 'region', split_axis=0, concat_axis=0, tiled=True)]
    ppermute x10 -> x8, starting transfers between devices: 10.9 us -> 9.45 us  [swap(): return lax.ppermute(x, BOTH, [(i, i ^ k) for i in range(devices)])]
    reshape x1 -> x0, local copies, waits for them, and re-layouts: 1.42 us -> none  [body(): measurement_ordering.reshape(1, count)]
    optimization_barrier x0 -> x1, local copies, waits for them, and re-layouts: none -> 1.09 us  [exchange(): total, state = lax.optimization_barrier((total, state))]
    transpose x1 -> x0, local copies, waits for them, and re-layouts: 1.09 us -> none  [body(): jnp.transpose(state, (2, 1, 0, 3))]
  transfers between devices with their start and end apart: 11 -> 9, of which waited for: 8 -> 7; matrix products, arithmetic and copies ran while one was open for 0% -> 0% of each run, Pallas kernels for 27% -> 26%
where the time goes in v2:
time: 58.7 us; the launch traced here: 58.5 us
  waiting for transfers between devices  21.2 us (36%)
  Pallas kernels  18 us (31%)
  starting transfers between devices  15.3 us (26%)
  local copies, waits for them, and re-layouts  3.18 us (5%)
  matrix products  0.75 us (1%)
    ppermute x8, waiting for transfers between devices, swap(): return lax.ppermute(x, BOTH, [(i, i ^ k) for i in range(devices)])  21.1 us
    pallas_call x1, Pallas kernels, body(): pl.pallas_call(functools.partial(filter_kernel, members), out_shape=[jax....  15.3 us
    ppermute x8, starting transfers between devices, swap(): return lax.ppermute(x, BOTH, [(i, i ^ k) for i in range(devices)])  9.45 us
    all_to_all x1, starting transfers between devices, exchange(): lax.all_to_all(state, 'region', split_axis=0, concat_axis=0, tiled=True)  5.83 us
    pallas_call x1, Pallas kernels, body(): pl.pallas_call(prior_kernel, out_shape=(jax.ShapeDtypeStruct((half, count...  2.77 us
    convert_element_type x1, local copies, waits for them, and re-layouts, body(): result.reshape(members, levels, 1, pixels * region_count).astype(bf16)  1.31 us
  transfers between devices with their start and end apart: 9, of which 7 were waited for; matrix products, arithmetic and copies ran while one was open for 0% of the time, Pallas kernels for 26%

profile of v2, /device:TPU:0, one launch (start us, length us, event | category | flops | bytes accessed | tf_op | source)
XLA Modules:
  0.0 58.5 jit_solution(1897100190591999572)
XLA Ops:
  0.0 0.0 copy-start.2
  0.0 2.8 %shard_map.100 = (f32[40,256]{1,0:T(8,128)S(1)}, f32[40,256]{1,0:T(8,128)S(1)}, f32[8,256]{1,0:T(8,128)S(1)}) custom-call(s32[1]{0:T(128)} %bitcast.2.first_ref, s32[1]{0:T(128)} %bitcast.1.half_ref, f32[4]{0:T(128)} %refs_0_.1, f32[4]{0:T(128)} %refs_1_.1, s32[4]{0:T(128)} %home_ref.1, f32[4,8]{1,0:T(4,128)} %bitcast.20, s32[4,64]{1,0:T(4,128)} %refs_4_.1, ...), custom_call_target="tpu_custom_call" | custom-call | tf_op jit(solution)/shard_map/pallas_call | solution.py:318
  2.8 0.6 collective-permute-start
  3.3 0.9 %collective-permute-done = f32[40,256]{1,0:T(8,128)S(1)} collective-permute-done((f32[40,256]{1,0:T(8,128)S(1)}, f32[40,256]{1,0:T(8,128)S(1)}, u32[]{:S(2)}, u32[]{:S(2)}) %collective-permute-start) | collective-permute-done | bytes 40992 | tf_op jit(solution)/shard_map/ppermute | solution.py:254
  4.2 3.8 %collective-permute-start.3 = (f32[40,256]{1,0:T(8,128)S(1)}, f32[40,256]{1,0:T(8,128)S(1)}, u32[]{:S(2)}, u32[]{:S(2)}) collective-permute-start(f32[40,256]{1,0:T(8,128)S(1)} %add.33), channel_id=1, source_target_pairs={{0,6},{1,7},{2,4},{3,5},{4,2},{5,3},{6,0},{7,1},{8,14},{9,15},{10,... | collective-permute-start | bytes 122888 | tf_op jit(solution)/shard_map/ppermute | solution.py:254
  8.0 0.5 collective-permute-start.2
  8.5 0.1 collective-permute-start.1
  8.6 1.3 %collective-permute-done.3 = f32[40,256]{1,0:T(8,128)S(1)} collective-permute-done((f32[40,256]{1,0:T(8,128)S(1)}, f32[40,256]{1,0:T(8,128)S(1)}, u32[]{:S(2)}, u32[]{:S(2)}) %collective-permute-start.3) | collective-permute-done | bytes 40992 | tf_op jit(solution)/shard_map/ppermute | solution.py:254
  10.0 2.0 %collective-permute-done.2 = f32[40,256]{1,0:T(8,128)S(1)} collective-permute-done((f32[40,256]{1,0:T(8,128)S(1)}, f32[40,256]{1,0:T(8,128)S(1)}, u32[]{:S(2)}, u32[]{:S(2)}) %collective-permute-start.2) | collective-permute-done | bytes 40992 | tf_op jit(solution)/shard_map/ppermute | solution.py:254
  12.0 0.5 collective-permute-done.1
  12.5 0.0 copy-done.2
  12.5 0.0 copy-start
  12.5 0.0 copy-start.1
  12.6 1.1 %copy.14 = bf16[8,4,80,128]{3,1,2,0:T(4,128)(2,1)} copy(bf16[8,4,80,128]{3,0,1,2:T(8,128)(2,1)S(1)} %bitcast.18) | data formatting | bytes 1310720 | tf_op jit(solution)/shard_map/optimization_barrier | solution.py:267
  13.6 5.8 %all-to-all-start = ((bf16[8,4,80,128]{3,1,2,0:T(4,128)(2,1)}), bf16[8,4,80,128]{3,1,2,0:T(4,128)(2,1)S(1)}, u32[]{:S(2)}, u32[]{:S(2)}) async-start(bf16[8,4,80,128]{3,1,2,0:T(4,128)(2,1)} %copy.14), calls=%async_computation | async-start | bytes 1310720 | tf_op jit(solution)/shard_map/all_to_all | solution.py:269
  19.5 3.8 %collective-permute-start.6 = (f32[40,256]{1,0:T(8,128)S(1)}, f32[40,256]{1,0:T(8,128)S(1)}, u32[]{:S(2)}, u32[]{:S(2)}) collective-permute-start(f32[40,256]{1,0:T(8,128)S(1)} %add_add_fusion.1), channel_id=1, source_target_pairs={{0,24},{1,25},{2,26},{3,27},{4,28},{5,29},{6,30},{7,31},{8,16},{9,... | collective-permute-start | bytes 122888 | tf_op jit(solution)/shard_map/ppermute | solution.py:254
  23.3 0.0 collective-permute-start.5
  23.3 0.6 collective-permute-start.4
  23.9 10.8 %collective-permute-done.6 = f32[40,256]{1,0:T(8,128)S(1)} collective-permute-done((f32[40,256]{1,0:T(8,128)S(1)}, f32[40,256]{1,0:T(8,128)S(1)}, u32[]{:S(2)}, u32[]{:S(2)}) %collective-permute-start.6) | collective-permute-done | bytes 40992 | tf_op jit(solution)/shard_map/ppermute | solution.py:254
  34.7 4.4 %collective-permute-done.5 = f32[40,256]{1,0:T(8,128)S(1)} collective-permute-done((f32[40,256]{1,0:T(8,128)S(1)}, f32[40,256]{1,0:T(8,128)S(1)}, u32[]{:S(2)}, u32[]{:S(2)}) %collective-permute-start.5) | collective-permute-done | bytes 40992 | tf_op jit(solution)/shard_map/ppermute | solution.py:254
  39.1 0.0 collective-permute-done.4
  39.1 0.1 collective-permute-start.7
  39.2 1.2 %collective-permute-done.7.other_ref = f32[40,256]{1,0:T(8,128)S(1)} collective-permute-done((f32[40,256]{1,0:T(8,128)S(1)}, f32[40,256]{1,0:T(8,128)S(1)}, u32[]{:S(2)}, u32[]{:S(2)}) %collective-permute-start.7) | collective-permute-done | bytes 40992 | tf_op jit(solution)/shard_map/ppermute | solution.py:254
  40.4 0.0 copy-done
  40.4 0.0 copy-done.1
  40.4 15.3 %shard_map.101 = (bf16[80,128]{1,0:T(8,128)(2,1)S(1)}, bf16[80,128]{1,0:T(8,128)(2,1)S(1)}) custom-call(s32[1]{0:T(128)} %bitcast.own_ref, s32[1]{0:T(128)} %bitcast.1.half_ref, s32[4]{0:T(128)S(1)} %copy-done, s32[8]{0:T(128)S(1)} %copy-done.1, f32[40,256]{1,0:T(8,128)S(1)} %add_add_fusion.mine_ref, f32[40,256]{1,0:T(8,128)S(1)} %collective-permute-done.7.other_ref, ...), custom_call_target="tpu_custom_call" | custom-call | flops 1000000000 | bytes 1000000 | tf_op jit(solution)/shard_map/pallas_call | solution.py:337
  55.7 0.0 all-to-all-done
  55.7 0.8 %copy.15 = bf16[80,4,8,128]{3,2,1,0:T(8,128)(2,1)S(1)} copy(bf16[80,4,8,128]{3,1,0,2:T(4,128)(2,1)S(1)} %bitcast.19) | data formatting | bytes 1310720 | tf_op jit(solution)/shard_map/transpose | solution.py:351
  56.5 0.4 fusion.1
  56.8 0.4 fusion
  57.2 1.3 %convert_element_type.15 = bf16[80,4,1,1024]{3,1,0,2:T(4,128)(2,1)} reshape(bf16[80,4096]{1,0:T(8,128)(2,1)S(1)} %fusion) | data formatting | bytes 1310720 | tf_op jit(solution)/shard_map/convert_element_type | solution.py:353
  (3 shorter events, 0.0 us)
Async XLA Ops:
  0.0 12.5 %copy-start.2 = (bf16[80,4,128,8]{2,3,1,0:T(8,128)(2,1)S(1)}, bf16[80,4,128,8]{2,3,1,0:T(8,128)(2,1)}, u32[]{:S(2)}) copy-start(bf16[80,4,128,8]{2,3,1,0:T(8,128)(2,1)} %param.10) | copy-start | bytes 1966084
  2.8 1.4 %collective-permute-start = (f32[40,256]{1,0:T(8,128)S(1)}, f32[40,256]{1,0:T(8,128)S(1)}, u32[]{:S(2)}, u32[]{:S(2)}) collective-permute-start(f32[40,256]{1,0:T(8,128)S(1)} %get-tuple-element.15), channel_id=1, source_target_pairs={{0,1},{1,0},{2,3},{3,2},{4,5},{5,4},{6,7},{7,6},{8,9},{9,8},{10,11... | collective-permute-start | bytes 122888 | tf_op jit(solution)/shard_map/ppermute | solution.py:254
  4.2 5.8 %collective-permute-start.3 = (f32[40,256]{1,0:T(8,128)S(1)}, f32[40,256]{1,0:T(8,128)S(1)}, u32[]{:S(2)}, u32[]{:S(2)}) collective-permute-start(f32[40,256]{1,0:T(8,128)S(1)} %add.33), channel_id=1, source_target_pairs={{0,6},{1,7},{2,4},{3,5},{4,2},{5,3},{6,0},{7,1},{8,14},{9,15},{10,... | collective-permute-start | bytes 122888 | tf_op jit(solution)/shard_map/ppermute | solution.py:254
  8.0 4.0 %collective-permute-start.2 = (f32[40,256]{1,0:T(8,128)S(1)}, f32[40,256]{1,0:T(8,128)S(1)}, u32[]{:S(2)}, u32[]{:S(2)}) collective-permute-start(f32[40,256]{1,0:T(8,128)S(1)} %add.33), channel_id=1, source_target_pairs={{0,4},{1,5},{2,6},{3,7},{4,0},{5,1},{6,2},{7,3},{8,12},{9,13},{10,... | collective-permute-start | bytes 122888 | tf_op jit(solution)/shard_map/ppermute | solution.py:254
  8.5 4.0 %collective-permute-start.1 = (f32[40,256]{1,0:T(8,128)S(1)}, f32[40,256]{1,0:T(8,128)S(1)}, u32[]{:S(2)}, u32[]{:S(2)}) collective-permute-start(f32[40,256]{1,0:T(8,128)S(1)} %add.33), channel_id=1, source_target_pairs={{0,2},{1,3},{2,0},{3,1},{4,6},{5,7},{6,4},{7,5},{8,10},{9,11},{10,... | collective-permute-start | bytes 122888 | tf_op jit(solution)/shard_map/ppermute | solution.py:254
  12.5 27.9 %copy-start = (s32[4]{0:T(128)S(1)}, s32[4]{0:T(128)}, u32[]{:S(2)}) copy-start(s32[4]{0:T(128)} %home_ref.1) | copy-start | bytes 52
  12.5 27.9 %copy-start.1 = (s32[8]{0:T(128)S(1)}, s32[8]{0:T(128)}, u32[]{:S(2)}) copy-start(s32[8]{0:T(128)} %radius_ref.1) | copy-start | bytes 100
  13.6 42.0 %all-to-all-start = ((bf16[8,4,80,128]{3,1,2,0:T(4,128)(2,1)}), bf16[8,4,80,128]{3,1,2,0:T(4,128)(2,1)S(1)}, u32[]{:S(2)}, u32[]{:S(2)}) async-start(bf16[8,4,80,128]{3,1,2,0:T(4,128)(2,1)} %copy.14), calls=%async_computation | async-start | bytes 1310720 | tf_op jit(solution)/shard_map/all_to_all | solution.py:269
  19.5 15.2 %collective-permute-start.6 = (f32[40,256]{1,0:T(8,128)S(1)}, f32[40,256]{1,0:T(8,128)S(1)}, u32[]{:S(2)}, u32[]{:S(2)}) collective-permute-start(f32[40,256]{1,0:T(8,128)S(1)} %add_add_fusion.1), channel_id=1, source_target_pairs={{0,24},{1,25},{2,26},{3,27},{4,28},{5,29},{6,30},{7,31},{8,16},{9,... | collective-permute-start | bytes 122888 | tf_op jit(solution)/shard_map/ppermute | solution.py:254
  23.3 15.8 %collective-permute-start.5 = (f32[40,256]{1,0:T(8,128)S(1)}, f32[40,256]{1,0:T(8,128)S(1)}, u32[]{:S(2)}, u32[]{:S(2)}) collective-permute-start(f32[40,256]{1,0:T(8,128)S(1)} %add_add_fusion.1), channel_id=1, source_target_pairs={{0,16},{1,17},{2,18},{3,19},{4,20},{5,21},{6,22},{7,23},{8,24},{9,... | collective-permute-start | bytes 122888 | tf_op jit(solution)/shard_map/ppermute | solution.py:254
  23.3 15.8 %collective-permute-start.4 = (f32[40,256]{1,0:T(8,128)S(1)}, f32[40,256]{1,0:T(8,128)S(1)}, u32[]{:S(2)}, u32[]{:S(2)}) collective-permute-start(f32[40,256]{1,0:T(8,128)S(1)} %add_add_fusion.1), channel_id=1, source_target_pairs={{0,8},{1,9},{2,10},{3,11},{4,12},{5,13},{6,14},{7,15},{8,0},{9,1},... | collective-permute-start | bytes 122888 | tf_op jit(solution)/shard_map/ppermute | solution.py:254
  39.1 1.3 %collective-permute-start.7 = (f32[40,256]{1,0:T(8,128)S(1)}, f32[40,256]{1,0:T(8,128)S(1)}, u32[]{:S(2)}, u32[]{:S(2)}) collective-permute-start(f32[40,256]{1,0:T(8,128)S(1)} %add_add_fusion.mine_ref), channel_id=1, source_target_pairs={{0,1},{1,0},{2,3},{3,2},{4,5},{5,4},{6,7},{7,6},{8,9},{9,8},{10,11... | collective-permute-start | bytes 122888 | tf_op jit(solution)/shard_map/ppermute | solution.py:254

commit v3 on v2

--- a/solution.py
+++ b/solution.py
@@ -21,6 +21,14 @@
 def dot(a, b, ca, cb, precision=highest):
     return lax.dot_general(
         a, b, (((ca,), (cb,)), ((), ())), precision=precision, preferred_element_type=f32
+    )
+
+
+def dot3(a, b, ca, cb):
+    a_hi, b_hi = a.astype(bf16), b.astype(bf16)
+    a_lo, b_lo = (a - a_hi.astype(f32)).astype(bf16), (b - b_hi.astype(f32)).astype(bf16)
+    return dot(a_hi, b_hi, ca, cb, None) + (
+        dot(a_hi, b_lo, ca, cb, None) + dot(a_lo, b_hi, ca, cb, None)
     )
 
 
@@ -112,12 +120,14 @@
 
 
 def col(x, j):
-    return jnp.broadcast_to(x[:, j : j + 1], (SUB, LANES))
+    if x.shape[1] < LANES:
+        x = jnp.concatenate([x, jnp.zeros((SUB, LANES - x.shape[1]), f32)], axis=1)
+    return jnp.take_along_axis(x, jnp.full((SUB, LANES), j, jnp.int32), axis=1)
 
 
 def filter_kernel(
     members, own_ref, half_ref, home_ref, radius_ref, mine_ref, other_ref, aux_ref, high_ref, low_ref,
-    x_ref, h_ref, b_ref,
+    x_ref, h_ref, b_ref, row_ref, pair_ref,
 ):
     padded, count = 2 * mine_ref.shape[0], mine_ref.shape[1]
     batches = home_ref.shape[0]
@@ -181,18 +191,22 @@
                 for i in range(j + 1, SUB):
                     for k in range(j + 1, i + 1):
                         s[i][k] = s[i][k] - l[i][j] * s[k][j]
-            U, H, alpha = [], [], []
+            U, alpha = [], []
+            scaled = []
+            pair_ref[:, :size] = G[p]
+            pair_ref[:, LANES:] = X[p]
             for j in range(SUB):
-                inv_alpha = 1.0 + jnp.sqrt(rep(noise_p[j : j + 1]) * inv[j])
+                share = rep(noise_p[j : j + 1]) * inv[j]
+                inv_alpha = 1.0 + share * lax.rsqrt(share)
                 alpha.append(1.0 / inv_alpha)
-                u = rep(G[p][j : j + 1])
-                h = rep(X[p][j : j + 1])
+                u = rep(pair_ref[j : j + 1, :size])
+                h = rep(pair_ref[j : j + 1, LANES:])
                 for i in range(j):
                     u = u - l[j][i][:, :size] * U[i]
-                    h = h - (l[j][i] * alpha[i]) * H[i]
+                    h = h - l[j][i] * scaled[i]
                 h = jnp.where(lane == E, h * inv_alpha, h)
                 U.append(u)
-                H.append(h)
+                scaled.append(alpha[j] * h)
                 row = jnp.where(lane == E + 1, alpha[j] * inv[j], h)
                 h_ref[SUB * p + j : SUB * p + j + 1] = row[:1]
             for g in range(p + 1, groups):
@@ -204,15 +218,15 @@
                     L.append(c * inv[j])
                 for j in range(SUB):
                     G[g] = G[g] - L[j][:, :size] * U[j]
-                    X[g] = X[g] - (L[j] * alpha[j]) * H[j]
+                    X[g] = X[g] - L[j] * scaled[j]
 
         low = min((r0 + size) // LANES * LANES, count)
         span = wide - low
         hb = h_ref[...]
         hm = jnp.where(member, hb, 0.0)
-        overlap = dot(hm, hm, 1, 1)
+        overlap = dot3(hm, hm, 1, 1)
         xr = x_ref[low:]
-        W = dot(hm, xr, 1, 1)
+        W = dot3(hm, xr, 1, 1)
         far = jnp.abs(owner[:, low:] - home_ref[b]).astype(f32)
         taper = jnp.maximum(0.0, 1.0 - far * inverse_cut[r0 : r0 + size]) * hb[:, E + 1 : E + 2]
         S = [overlap[SUB * g : SUB * g + SUB] for g in range(groups)]
@@ -227,8 +241,9 @@
         for p in range(groups):
             C = [[col(S[g], SUB * p + j) for g in range(p, groups)] for j in range(SUB)]
             B = []
+            row_ref[:, : LANES * tiles] = W[p]
             for j in range(SUB):
-                w = rep(W[p][j : j + 1])
+                w = rep(row_ref[j : j + 1, : LANES * tiles])
                 for i in range(j):
                     w = w - scale(rep(C[i][0][j : j + 1]), B[i])
                 beta = w * rep(taper[SUB * p + j : SUB * p + j + 1])
@@ -237,7 +252,7 @@
             for g in range(p + 1, groups):
                 for j in range(SUB):
                     W[g] = W[g] - scale(C[j][g - p], B[j])
-        x_ref[low:] = xr - dot(b_ref[:, low:], hb, 0, 0)
+        x_ref[low:] = xr - dot3(b_ref[:, low:], hb, 0, 0)
 
     last = x_ref[count : count + members]
     mixing = jnp.where(member, last + last[:, E : E + 1], 0.0)
@@ -256,23 +271,15 @@
 
 def exchange(keep, send, state, devices):
     total = keep + swap(send, devices, 1)
+    total, state = lax.optimization_barrier((total, state))
+    state = jnp.transpose(state, (2, 1, 0, 3))
     bit = 2
     while bit < devices:
-        last = 4 * bit >= devices
         steps = (bit, 2 * bit, 3 * bit) if 2 * bit < devices else (bit,)
-        if bit == 2:
-            total, state = lax.optimization_barrier((total, state))
-            state = jnp.transpose(state, (2, 1, 0, 3))
-        if last:
-            total, state = lax.optimization_barrier((total, state))
-            moved = [swap(total, devices, k) for k in steps]
-            whole = lax.all_to_all(
-                state, "region", split_axis=0, concat_axis=0, tiled=True
-            )
-        else:
-            moved = [swap(total, devices, k) for k in steps]
+        moved = [swap(total, devices, k) for k in steps]
         total = total + sum(moved)
         bit *= 4
+    whole = lax.all_to_all(state, "region", split_axis=0, concat_axis=0, tiled=True)
     return total, swap(total, devices, 1), whole
 
 
@@ -343,6 +350,8 @@
             pltpu.VMEM((count + LANES, LANES), f32),
             pltpu.VMEM((size, LANES), f32),
             pltpu.VMEM((size, count + LANES), f32),
+            pltpu.VMEM((SUB, count + LANES), f32),
+            pltpu.VMEM((SUB, 2 * LANES), f32),
         ],
         compiler_params=pltpu.CompilerParams(vmem_limit_bytes=16 * 2**20),
         cost_estimate=pl.CostEstimate(flops=10**9, bytes_accessed=10**6, transcendentals=0),

time: 58.7 us -> 51.4 us (0.88)
  waiting for transfers between devices: 21.2 us -> 14.8 us
  Pallas kernels: 18 us -> 15.1 us
  local copies, waits for them, and re-layouts: 3.18 us -> 4.28 us
  starting transfers between devices: 15.3 us -> 16.2 us
    ppermute x8, waiting for transfers between devices: 21.1 us -> 14.8 us  [swap(): return lax.ppermute(x, BOTH, [(i, i ^ k) for i in range(devices)])]
    pallas_call x1, Pallas kernels: 15.3 us -> 12.4 us  [body(): pl.pallas_call(functools.partial(filter_kernel, members), out_shape=[jax....]
    transpose x0 -> x1, local copies, waits for them, and re-layouts: none -> 2.19 us  [exchange(): state = jnp.transpose(state, (2, 1, 0, 3))]
    all_to_all x1, starting transfers between devices: 5.83 us -> 7.17 us  [exchange(): lax.all_to_all(state, 'region', split_axis=0, concat_axis=0, tiled=True)]
    optimization_barrier x1 -> x0, local copies, waits for them, and re-layouts: 1.09 us -> none  [exchange(): total, state = lax.optimization_barrier((total, state))]
  transfers between devices with their start and end apart: 9 -> 9, of which waited for: 7 -> 6; matrix products, arithmetic and copies ran while one was open for 0% -> 0% of each run, Pallas kernels for 26% -> 24%
where the time goes in v3:
time: 51.4 us; the launch traced here: 51.2 us
  starting transfers between devices  16.2 us (32%)
  Pallas kernels  15.1 us (29%)
  waiting for transfers between devices  14.8 us (29%)
  local copies, waits for them, and re-layouts  4.28 us (8%)
  matrix products  0.75 us (1%)
    ppermute x8, waiting for transfers between devices, swap(): return lax.ppermute(x, BOTH, [(i, i ^ k) for i in range(devices)])  14.8 us
    pallas_call x1, Pallas kernels, body(): pl.pallas_call(functools.partial(filter_kernel, members), out_shape=[jax....  12.4 us
    ppermute x8, starting transfers between devices, swap(): return lax.ppermute(x, BOTH, [(i, i ^ k) for i in range(devices)])  9.04 us
    all_to_all x1, starting transfers between devices, exchange(): lax.all_to_all(state, 'region', split_axis=0, concat_axis=0, tiled=True)  7.17 us
    pallas_call x1, Pallas kernels, body(): pl.pallas_call(prior_kernel, out_shape=(jax.ShapeDtypeStruct((half, count...  2.7 us
    transpose x1, local copies, waits for them, and re-layouts, exchange(): state = jnp.transpose(state, (2, 1, 0, 3))  2.19 us
    convert_element_type x1, local copies, waits for them, and re-layouts, body(): result.reshape(members, levels, 1, pixels * region_count).astype(bf16)  1.31 us
  transfers between devices with their start and end apart: 9, of which 6 were waited for; matrix products, arithmetic and copies ran while one was open for 0% of the time, Pallas kernels for 24%

profile of v3, /device:TPU:0, one launch (start us, length us, event | category | flops | bytes accessed | tf_op | source)
XLA Modules:
  0.0 51.2 jit_solution(80383567363911115)
XLA Ops:
  0.0 2.7 %shard_map.100 = (f32[40,256]{1,0:T(8,128)S(1)}, f32[40,256]{1,0:T(8,128)S(1)}, f32[8,256]{1,0:T(8,128)S(1)}) custom-call(s32[1]{0:T(128)} %bitcast.2.first_ref, s32[1]{0:T(128)} %bitcast.1.half_ref, f32[4]{0:T(128)} %refs_0_.1, f32[4]{0:T(128)} %refs_1_.1, s32[4]{0:T(128)} %home_ref.1, f32[4,8]{1,0:T(4,128)} %bitcast.20, s32[4,64]{1,0:T(4,128)} %refs_4_.1, ...), custom_call_target="tpu_custom_call" | custom-call | tf_op jit(solution)/shard_map/pallas_call | solution.py:325
  2.7 0.6 %collective-permute-start = (f32[40,256]{1,0:T(8,128)S(1)}, f32[40,256]{1,0:T(8,128)S(1)}, u32[]{:S(2)}, u32[]{:S(2)}) collective-permute-start(f32[40,256]{1,0:T(8,128)S(1)} %get-tuple-element.13), channel_id=1, source_target_pairs={{0,1},{1,0},{2,3},{3,2},{4,5},{5,4},{6,7},{7,6},{8,9},{9,8},{10,11... | collective-permute-start | bytes 122888 | tf_op jit(solution)/shard_map/ppermute | solution.py:269
  3.3 0.9 %collective-permute-done = f32[40,256]{1,0:T(8,128)S(1)} collective-permute-done((f32[40,256]{1,0:T(8,128)S(1)}, f32[40,256]{1,0:T(8,128)S(1)}, u32[]{:S(2)}, u32[]{:S(2)}) %collective-permute-start) | collective-permute-done | bytes 40992 | tf_op jit(solution)/shard_map/ppermute | solution.py:269
  4.1 0.0 copy-start
  4.2 0.0 copy-start.1
  4.2 2.2 %copy.14 = bf16[8,4,80,128]{3,1,2,0:T(4,128)(2,1)} copy(bf16[8,4,80,128]{3,0,1,2:T(8,128)(2,1)} %bitcast.18) | data formatting | bytes 1310720 | tf_op jit(solution)/shard_map/transpose | solution.py:275
  6.4 7.2 %all-to-all-start = ((bf16[8,4,80,128]{3,1,2,0:T(4,128)(2,1)}), bf16[8,4,80,128]{3,1,2,0:T(4,128)(2,1)S(1)}, u32[]{:S(2)}, u32[]{:S(2)}) async-start(bf16[8,4,80,128]{3,1,2,0:T(4,128)(2,1)} %copy.14), calls=%async_computation | async-start | bytes 1310720 | tf_op jit(solution)/shard_map/all_to_all | solution.py:282
  13.5 2.9 %collective-permute-start.3 = (f32[40,256]{1,0:T(8,128)S(1)}, f32[40,256]{1,0:T(8,128)S(1)}, u32[]{:S(2)}, u32[]{:S(2)}) collective-permute-start(f32[40,256]{1,0:T(8,128)S(1)} %add.33), channel_id=1, source_target_pairs={{0,6},{1,7},{2,4},{3,5},{4,2},{5,3},{6,0},{7,1},{8,14},{9,15},{10,... | collective-permute-start | bytes 122888 | tf_op jit(solution)/shard_map/ppermute | solution.py:269
  16.5 0.0 collective-permute-start.2
  16.5 0.6 %collective-permute-start.1 = (f32[40,256]{1,0:T(8,128)S(1)}, f32[40,256]{1,0:T(8,128)S(1)}, u32[]{:S(2)}, u32[]{:S(2)}) collective-permute-start(f32[40,256]{1,0:T(8,128)S(1)} %add.33), channel_id=1, source_target_pairs={{0,2},{1,3},{2,0},{3,1},{4,6},{5,7},{6,4},{7,5},{8,10},{9,11},{10,... | collective-permute-start | bytes 122888 | tf_op jit(solution)/shard_map/ppermute | solution.py:269
  17.0 2.0 %collective-permute-done.3 = f32[40,256]{1,0:T(8,128)S(1)} collective-permute-done((f32[40,256]{1,0:T(8,128)S(1)}, f32[40,256]{1,0:T(8,128)S(1)}, u32[]{:S(2)}, u32[]{:S(2)}) %collective-permute-start.3) | collective-permute-done | bytes 40992 | tf_op jit(solution)/shard_map/ppermute | solution.py:269
  19.0 3.9 %collective-permute-done.2 = f32[40,256]{1,0:T(8,128)S(1)} collective-permute-done((f32[40,256]{1,0:T(8,128)S(1)}, f32[40,256]{1,0:T(8,128)S(1)}, u32[]{:S(2)}, u32[]{:S(2)}) %collective-permute-start.2) | collective-permute-done | bytes 40992 | tf_op jit(solution)/shard_map/ppermute | solution.py:269
  22.9 0.0 collective-permute-done.1
  22.9 4.3 %collective-permute-start.6 = (f32[40,256]{1,0:T(8,128)S(1)}, f32[40,256]{1,0:T(8,128)S(1)}, u32[]{:S(2)}, u32[]{:S(2)}) collective-permute-start(f32[40,256]{1,0:T(8,128)S(1)} %add_add_fusion.1), channel_id=1, source_target_pairs={{0,24},{1,25},{2,26},{3,27},{4,28},{5,29},{6,30},{7,31},{8,16},{9,... | collective-permute-start | bytes 122888 | tf_op jit(solution)/shard_map/ppermute | solution.py:269
  27.2 0.0 collective-permute-start.5
  27.2 0.6 %collective-permute-start.4 = (f32[40,256]{1,0:T(8,128)S(1)}, f32[40,256]{1,0:T(8,128)S(1)}, u32[]{:S(2)}, u32[]{:S(2)}) collective-permute-start(f32[40,256]{1,0:T(8,128)S(1)} %add_add_fusion.1), channel_id=1, source_target_pairs={{0,8},{1,9},{2,10},{3,11},{4,12},{5,13},{6,14},{7,15},{8,0},{9,1},... | collective-permute-start | bytes 122888 | tf_op jit(solution)/shard_map/ppermute | solution.py:269
  27.8 2.0 %collective-permute-done.6 = f32[40,256]{1,0:T(8,128)S(1)} collective-permute-done((f32[40,256]{1,0:T(8,128)S(1)}, f32[40,256]{1,0:T(8,128)S(1)}, u32[]{:S(2)}, u32[]{:S(2)}) %collective-permute-start.6) | collective-permute-done | bytes 40992 | tf_op jit(solution)/shard_map/ppermute | solution.py:269
  29.9 4.8 %collective-permute-done.5 = f32[40,256]{1,0:T(8,128)S(1)} collective-permute-done((f32[40,256]{1,0:T(8,128)S(1)}, f32[40,256]{1,0:T(8,128)S(1)}, u32[]{:S(2)}, u32[]{:S(2)}) %collective-permute-start.5) | collective-permute-done | bytes 40992 | tf_op jit(solution)/shard_map/ppermute | solution.py:269
  34.7 0.0 collective-permute-done.4
  34.7 0.1 collective-permute-start.7
  34.8 1.2 %collective-permute-done.7.other_ref = f32[40,256]{1,0:T(8,128)S(1)} collective-permute-done((f32[40,256]{1,0:T(8,128)S(1)}, f32[40,256]{1,0:T(8,128)S(1)}, u32[]{:S(2)}, u32[]{:S(2)}) %collective-permute-start.7) | collective-permute-done | bytes 40992 | tf_op jit(solution)/shard_map/ppermute | solution.py:269
  36.0 0.0 copy-done
  36.0 0.0 copy-done.1
  36.0 12.4 %shard_map.101 = (bf16[80,128]{1,0:T(8,128)(2,1)S(1)}, bf16[80,128]{1,0:T(8,128)(2,1)S(1)}) custom-call(s32[1]{0:T(128)} %bitcast.own_ref, s32[1]{0:T(128)} %bitcast.1.half_ref, s32[4]{0:T(128)S(1)} %copy-done, s32[8]{0:T(128)S(1)} %copy-done.1, f32[40,256]{1,0:T(8,128)S(1)} %add_add_fusion.mine_ref, f32[40,256]{1,0:T(8,128)S(1)} %collective-permute-done.7.other_ref, ...), custom_call_target="tpu_custom_call" | custom-call | flops 1000000000 | bytes 1000000 | tf_op jit(solution)/shard_map/pallas_call | solution.py:344
  48.3 0.0 all-to-all-done
  48.3 0.8 %copy.15 = bf16[80,4,8,128]{3,2,1,0:T(8,128)(2,1)S(1)} copy(bf16[80,4,8,128]{3,1,0,2:T(4,128)(2,1)S(1)} %bitcast.19) | data formatting | bytes 1310720 | tf_op jit(solution)/shard_map/transpose | solution.py:360
  49.1 0.4 fusion.1
  49.5 0.4 fusion
  49.9 1.3 %convert_element_type.15 = bf16[80,4,1,1024]{3,1,0,2:T(4,128)(2,1)} reshape(bf16[80,4096]{1,0:T(8,128)(2,1)S(1)} %fusion) | data formatting | bytes 1310720 | tf_op jit(solution)/shard_map/convert_element_type | solution.py:362
  (3 shorter events, 0.0 us)
Async XLA Ops:
  2.7 1.4 %collective-permute-start = (f32[40,256]{1,0:T(8,128)S(1)}, f32[40,256]{1,0:T(8,128)S(1)}, u32[]{:S(2)}, u32[]{:S(2)}) collective-permute-start(f32[40,256]{1,0:T(8,128)S(1)} %get-tuple-element.13), channel_id=1, source_target_pairs={{0,1},{1,0},{2,3},{3,2},{4,5},{5,4},{6,7},{7,6},{8,9},{9,8},{10,11... | collective-permute-start | bytes 122888 | tf_op jit(solution)/shard_map/ppermute | solution.py:269
  4.1 31.8 %copy-start = (s32[4]{0:T(128)S(1)}, s32[4]{0:T(128)}, u32[]{:S(2)}) copy-start(s32[4]{0:T(128)} %home_ref.1) | copy-start | bytes 52
  4.2 31.8 %copy-start.1 = (s32[8]{0:T(128)S(1)}, s32[8]{0:T(128)}, u32[]{:S(2)}) copy-start(s32[8]{0:T(128)} %radius_ref.1) | copy-start | bytes 100
  6.4 42.0 %all-to-all-start = ((bf16[8,4,80,128]{3,1,2,0:T(4,128)(2,1)}), bf16[8,4,80,128]{3,1,2,0:T(4,128)(2,1)S(1)}, u32[]{:S(2)}, u32[]{:S(2)}) async-start(bf16[8,4,80,128]{3,1,2,0:T(4,128)(2,1)} %copy.14), calls=%async_computation | async-start | bytes 1310720 | tf_op jit(solution)/shard_map/all_to_all | solution.py:282
  13.5 5.5 %collective-permute-start.3 = (f32[40,256]{1,0:T(8,128)S(1)}, f32[40,256]{1,0:T(8,128)S(1)}, u32[]{:S(2)}, u32[]{:S(2)}) collective-permute-start(f32[40,256]{1,0:T(8,128)S(1)} %add.33), channel_id=1, source_target_pairs={{0,6},{1,7},{2,4},{3,5},{4,2},{5,3},{6,0},{7,1},{8,14},{9,15},{10,... | collective-permute-start | bytes 122888 | tf_op jit(solution)/shard_map/ppermute | solution.py:269
  16.5 6.4 %collective-permute-start.2 = (f32[40,256]{1,0:T(8,128)S(1)}, f32[40,256]{1,0:T(8,128)S(1)}, u32[]{:S(2)}, u32[]{:S(2)}) collective-permute-start(f32[40,256]{1,0:T(8,128)S(1)} %add.33), channel_id=1, source_target_pairs={{0,4},{1,5},{2,6},{3,7},{4,0},{5,1},{6,2},{7,3},{8,12},{9,13},{10,... | collective-permute-start | bytes 122888 | tf_op jit(solution)/shard_map/ppermute | solution.py:269
  16.5 6.4 %collective-permute-start.1 = (f32[40,256]{1,0:T(8,128)S(1)}, f32[40,256]{1,0:T(8,128)S(1)}, u32[]{:S(2)}, u32[]{:S(2)}) collective-permute-start(f32[40,256]{1,0:T(8,128)S(1)} %add.33), channel_id=1, source_target_pairs={{0,2},{1,3},{2,0},{3,1},{4,6},{5,7},{6,4},{7,5},{8,10},{9,11},{10,... | collective-permute-start | bytes 122888 | tf_op jit(solution)/shard_map/ppermute | solution.py:269
  22.9 6.9 %collective-permute-start.6 = (f32[40,256]{1,0:T(8,128)S(1)}, f32[40,256]{1,0:T(8,128)S(1)}, u32[]{:S(2)}, u32[]{:S(2)}) collective-permute-start(f32[40,256]{1,0:T(8,128)S(1)} %add_add_fusion.1), channel_id=1, source_target_pairs={{0,24},{1,25},{2,26},{3,27},{4,28},{5,29},{6,30},{7,31},{8,16},{9,... | collective-permute-start | bytes 122888 | tf_op jit(solution)/shard_map/ppermute | solution.py:269
  27.2 7.5 %collective-permute-start.5 = (f32[40,256]{1,0:T(8,128)S(1)}, f32[40,256]{1,0:T(8,128)S(1)}, u32[]{:S(2)}, u32[]{:S(2)}) collective-permute-start(f32[40,256]{1,0:T(8,128)S(1)} %add_add_fusion.1), channel_id=1, source_target_pairs={{0,16},{1,17},{2,18},{3,19},{4,20},{5,21},{6,22},{7,23},{8,24},{9,... | collective-permute-start | bytes 122888 | tf_op jit(solution)/shard_map/ppermute | solution.py:269
  27.2 7.5 %collective-permute-start.4 = (f32[40,256]{1,0:T(8,128)S(1)}, f32[40,256]{1,0:T(8,128)S(1)}, u32[]{:S(2)}, u32[]{:S(2)}) collective-permute-start(f32[40,256]{1,0:T(8,128)S(1)} %add_add_fusion.1), channel_id=1, source_target_pairs={{0,8},{1,9},{2,10},{3,11},{4,12},{5,13},{6,14},{7,15},{8,0},{9,1},... | collective-permute-start | bytes 122888 | tf_op jit(solution)/shard_map/ppermute | solution.py:269
  34.7 1.3 %collective-permute-start.7 = (f32[40,256]{1,0:T(8,128)S(1)}, f32[40,256]{1,0:T(8,128)S(1)}, u32[]{:S(2)}, u32[]{:S(2)}) collective-permute-start(f32[40,256]{1,0:T(8,128)S(1)} %add_add_fusion.mine_ref), channel_id=1, source_target_pairs={{0,1},{1,0},{2,3},{3,2},{4,5},{5,4},{6,7},{7,6},{8,9},{9,8},{10,11... | collective-permute-start | bytes 122888 | tf_op jit(solution)/shard_map/ppermute | solution.py:269

commit v4 on v3

--- a/solution.py
+++ b/solution.py
@@ -46,7 +46,7 @@
 
 def prior_kernel(first_ref, half_ref, *refs):
     inputs, (keep_ref, send_ref, aux_ref), held, arrived = (
-        refs[:9], refs[9:12], refs[12:21], refs[21]
+        refs[:11], refs[11:14], refs[14:25], refs[25]
     )
     copies = [
         pltpu.make_async_copy(source, target, arrived.at[i])
@@ -56,7 +56,7 @@
         copy.start()
     for copy in copies[:-1]:
         copy.wait()
-    (down_ref, across_ref, home_ref, height_ref, order_ref, place_ref, amount_ref, noise_ref,
+    (down_ref, across_ref, home_ref, area_ref, radius_ref, height_ref, order_ref, place_ref, amount_ref, noise_ref,
      state_ref) = held
     members, levels, regions, pixels = state_ref.shape
     batches, size = order_ref.shape
@@ -74,10 +74,16 @@
     for ref in (place_ref, amount_ref, noise_ref):
         wide = dot(ref[...].astype(f32), spread, 0, 0)
         rows.append(jnp.sum(jnp.where(hit, wide, 0.0), axis=0, keepdims=True))
-    aux_ref[...] = jnp.concatenate(rows + [jnp.zeros((SUB - 3, count), f32)], axis=0)
-
     picked = rows[0].astype(jnp.int32)
     channel = picked // sites
+    cut = jnp.zeros((1, count), jnp.int32)
+    for c in range(channels):
+        cut = jnp.where(channel == c, radius_ref[c], cut)
+    area = jnp.zeros((1, count), jnp.int32)
+    for k in range(batches):
+        area = jnp.where(lane // size == k, area_ref[k], area)
+    rows += [cut.astype(f32), area.astype(f32), jnp.zeros((SUB - 5, count), f32)]
+    aux_ref[...] = jnp.concatenate(rows, axis=0)
     spot = picked - channel * sites
     spot_row = spot // (TILE // STRIDE)
     spot_col = spot - spot_row * (TILE // STRIDE)
@@ -126,15 +132,12 @@
 
 
 def filter_kernel(
-    members, own_ref, half_ref, home_ref, radius_ref, mine_ref, other_ref, aux_ref, high_ref, low_ref,
+    members, batches, own_ref, half_ref, mine_ref, other_ref, aux_ref, high_ref, low_ref,
     x_ref, h_ref, b_ref, row_ref, pair_ref,
 ):
     padded, count = 2 * mine_ref.shape[0], mine_ref.shape[1]
-    batches = home_ref.shape[0]
     size = count // batches
     groups = size // SUB
-    channels = radius_ref.shape[0]
-    sites = (TILE // STRIDE) * (TILE // STRIDE)
     dof = members - 1.0
     E = padded
     lane = iota((1, LANES), 1)
@@ -157,17 +160,12 @@
     square = iota((LANES, LANES), 0)
     x_ref[count:] = jnp.where((square == iota((LANES, LANES), 1)) & (square < members), 1.0, 0.0)
 
-    place = aux_cols[:, 0:1].astype(jnp.int32) // sites
-    cut = jnp.zeros((count, 1), f32)
-    for c in range(channels):
-        cut = jnp.where(place == c, radius_ref[c].astype(f32), cut)
-    inverse_cut = 1.0 / (cut + 1.0)
+    inverse_cut = 1.0 / (aux_cols[:, 3:4] + 1.0)
     noise = aux_cols[:, 2:3] * dof
 
     wide = count + LANES
-    owner = jnp.zeros((1, wide), jnp.int32) + own_ref[0]
-    for k in range(batches):
-        owner = jnp.where(iota((1, wide), 1) // size == k, home_ref[k], owner)
+    own = jnp.zeros((1, LANES), f32) + own_ref[0].astype(f32)
+    owner = jnp.concatenate([aux[4:5], own], axis=1)
 
     for b in range(batches):
         r0 = b * size
@@ -227,7 +225,7 @@
         overlap = dot3(hm, hm, 1, 1)
         xr = x_ref[low:]
         W = dot3(hm, xr, 1, 1)
-        far = jnp.abs(owner[:, low:] - home_ref[b]).astype(f32)
+        far = jnp.abs(owner[:, low:] - aux_cols[r0 : r0 + size, 4:5])
         taper = jnp.maximum(0.0, 1.0 - far * inverse_cut[r0 : r0 + size]) * hb[:, E + 1 : E + 2]
         S = [overlap[SUB * g : SUB * g + SUB] for g in range(groups)]
         W = [W[SUB * g : SUB * g + SUB] for g in range(groups)]
@@ -262,6 +260,20 @@
     low_ref[...] = (mixing - high.astype(f32)).astype(bf16)
 
 
+def apply_kernel(high_ref, low_ref, whole_ref, out_ref, row_ref):
+    sources, levels, members, pixels = whole_ref.shape
+    high, low = high_ref[:, :members], low_ref[:, :members]
+    for level in range(levels):
+        field = jnp.concatenate([whole_ref[s, level] for s in range(sources)], axis=1)
+        value = dot(high, field, 0, 0, None) + dot(low, field, 0, 0, None)
+        for s in range(sources):
+            part = value[:, pixels * s : pixels * s + pixels]
+            row_ref[s, pl.ds(level, members, stride=levels), :] = part
+    for s in range(sources):
+        part = row_ref[s].reshape(members, levels, pixels).astype(bf16)
+        out_ref[:, :, pixels * s : pixels * s + pixels] = part
+
+
 BOTH = ("region", "lev")
 
 
@@ -273,12 +285,15 @@
     total = keep + swap(send, devices, 1)
     total, state = lax.optimization_barrier((total, state))
     state = jnp.transpose(state, (2, 1, 0, 3))
-    bit = 2
+    stages = []
+    bit = 8
     while bit < devices:
-        steps = (bit, 2 * bit, 3 * bit) if 2 * bit < devices else (bit,)
+        stages.append((3 * bit, 2 * bit, bit) if 2 * bit < devices else (bit,))
+        bit *= 4
+    stages += [(k,) for k in (4, 2) if k < devices]
+    for steps in stages:
         moved = [swap(total, devices, k) for k in steps]
         total = total + sum(moved)
-        bit *= 4
     whole = lax.all_to_all(state, "region", split_axis=0, concat_axis=0, tiled=True)
     return total, swap(total, devices, 1), whole
 
@@ -313,7 +328,9 @@
     side = ((own_region * level_count + lax.axis_index("lev")) % 2).astype(jnp.int32)[None]
     vmem = pl.BlockSpec(memory_space=pltpu.VMEM)
     smem = pl.BlockSpec(memory_space=pltpu.SMEM)
-    scalars = (sensor_spread_down, sensor_spread_across, home)
+    scalars = (
+        sensor_spread_down, sensor_spread_across, home, group_area_number, taper_radius_limit
+    )
     tables = (
         jnp.transpose(channel_height_kernel),
         measurement_ordering,
@@ -329,11 +346,11 @@
             jax.ShapeDtypeStruct((half, count), f32),
             jax.ShapeDtypeStruct((SUB, count), f32),
         ),
-        in_specs=[smem] * 2 + [pl.BlockSpec(memory_space=pltpu.HBM)] * 9,
+        in_specs=[smem] * 2 + [pl.BlockSpec(memory_space=pltpu.HBM)] * 11,
         out_specs=(vmem, vmem, vmem),
         scratch_shapes=[pltpu.SMEM(x.shape, x.dtype) for x in scalars]
         + [pltpu.VMEM(x.shape, x.dtype) for x in tables]
-        + [pltpu.SemaphoreType.DMA((9,))],
+        + [pltpu.SemaphoreType.DMA((11,))],
         compiler_params=pltpu.CompilerParams(vmem_limit_bytes=24 * 2**20),
     )(
         (own_region * pixels)[None],
@@ -342,9 +359,9 @@
     )
     mine, other, whole = exchange(keep, send, state, devices)
     pieces = pl.pallas_call(
-        functools.partial(filter_kernel, members),
+        functools.partial(filter_kernel, members, batches),
         out_shape=[jax.ShapeDtypeStruct((members, LANES), bf16)] * 2,
-        in_specs=[smem] * 4 + [vmem] * 3,
+        in_specs=[smem] * 2 + [vmem] * 3,
         out_specs=[vmem, vmem],
         scratch_shapes=[
             pltpu.VMEM((count + LANES, LANES), f32),
@@ -355,8 +372,18 @@
         ],
         compiler_params=pltpu.CompilerParams(vmem_limit_bytes=16 * 2**20),
         cost_estimate=pl.CostEstimate(flops=10**9, bytes_accessed=10**6, transcendentals=0),
-    )(own_region[None], side, group_area_number, taper_radius_limit, mine, other, aux)
-
+    )(own_region[None], side, mine, other, aux)
+
+    if pixels % LANES == 0 and levels == 4:
+        result = pl.pallas_call(
+            apply_kernel,
+            out_shape=jax.ShapeDtypeStruct((members, levels, pixels * region_count), bf16),
+            in_specs=[vmem] * 3,
+            out_specs=vmem,
+            scratch_shapes=[pltpu.VMEM((region_count, members * levels, pixels), f32)],
+            compiler_params=pltpu.CompilerParams(vmem_limit_bytes=24 * 2**20),
+        )(*pieces, whole)
+        return result[:, :, None]
     field = jnp.transpose(whole, (2, 1, 0, 3)).reshape(members, -1)
     result = sum(dot(piece[:, :members], field, 0, 0, None) for piece in pieces)
     return result.reshape(members, levels, 1, pixels * region_count).astype(bf16)

time: 51.4 us -> 55.6 us (1.082)
  waiting for transfers between devices: 14.8 us -> 23.2 us
  local copies, waits for them, and re-layouts: 4.28 us -> 1.09 us
  starting transfers between devices: 16.2 us -> 14.9 us
  Pallas kernels: 15.1 us -> 16 us
  matrix products: 0.75 us -> 0 us
    ppermute x8 -> x7, waiting for transfers between devices: 14.8 us -> 23.2 us  [swap(): return lax.ppermute(x, BOTH, [(i, i ^ k) for i in range(devices)])]
    transpose x2 -> x0, local copies, waits for them, and re-layouts: 2.96 us -> none  [the longest x1 2.19 us: exchange(): state = jnp.transpose(state, (2, 1, 0, 3))]
    convert_element_type x1 -> x0, local copies, waits for them, and re-layouts: 1.31 us -> none  [body(): result.reshape(members, levels, 1, pixels * region_count).astype(bf16)]
    unnamed x4 -> x3, local copies, waits for them, and re-layouts: 0.01 us -> 1.09 us
    ppermute x8 -> x7, starting transfers between devices: 9.04 us -> 7.99 us  [swap(): return lax.ppermute(x, BOTH, [(i, i ^ k) for i in range(devices)])]
    pallas_call x1 -> x2, Pallas kernels: 12.4 us -> 13.2 us  [the longest x1 11.7 us: body(): pl.pallas_call(functools.partial(filter_kernel, members, batches), out_sh...]
    dot_general x2 -> x0, matrix products: 0.75 us -> none  [dot(): lax.dot_general(a, b, (((ca,), (cb,)), ((), ())), precision=precision, pr...]
  transfers between devices with their start and end apart: 9 -> 8, of which waited for: 6 -> 5; matrix products, arithmetic and copies ran while one was open for 0% -> 2% of each run, Pallas kernels for 24% -> 21%
where the time goes in v4:
time: 55.6 us; the launch traced here: 55.4 us
  waiting for transfers between devices  23.2 us (42%)
  Pallas kernels  16 us (29%)
  starting transfers between devices  14.9 us (27%)
  local copies, waits for them, and re-layouts  1.09 us (2%)
    ppermute x7, waiting for transfers between devices, swap(): return lax.ppermute(x, BOTH, [(i, i ^ k) for i in range(devices)])  23.2 us
    pallas_call x1, Pallas kernels, body(): pl.pallas_call(functools.partial(filter_kernel, members, batches), out_sh...  11.7 us
    ppermute x7, starting transfers between devices, swap(): return lax.ppermute(x, BOTH, [(i, i ^ k) for i in range(devices)])  7.99 us
    all_to_all x1, starting transfers between devices, exchange(): lax.all_to_all(state, 'region', split_axis=0, concat_axis=0, tiled=True)  6.94 us
    pallas_call x1, Pallas kernels, body(): pl.pallas_call(prior_kernel, out_shape=(jax.ShapeDtypeStruct((half, count...  2.81 us
    pallas_call x1, Pallas kernels, body(): pl.pallas_call(apply_kernel, out_shape=jax.ShapeDtypeStruct((members, lev...  1.54 us
  transfers between devices with their start and end apart: 8, of which 5 were waited for; matrix products, arithmetic and copies ran while one was open for 2% of the time, Pallas kernels for 21%

profile of v4, /device:TPU:0, one launch (start us, length us, event | category | flops | bytes accessed | tf_op | source)
XLA Modules:
  0.0 55.4 jit_solution(1769976919379244014)
XLA Ops:
  0.0 0.0 copy-start
  0.0 2.8 %shard_map.100 = (f32[40,256]{1,0:T(8,128)S(1)}, f32[40,256]{1,0:T(8,128)S(1)}, f32[8,256]{1,0:T(8,128)S(1)}) custom-call(s32[1]{0:T(128)} %bitcast.2.first_ref, s32[1]{0:T(128)} %bitcast.1.half_ref, f32[4]{0:T(128)} %refs_0_.1, f32[4]{0:T(128)} %refs_1_.1, s32[4]{0:T(128)} %refs_3_.1, s32[4]{0:T(128)} %refs_3_.1, s32[8]{0:T(128)} %refs_4_.1, ...), custom_call_target="tpu_custom_call" | custom-call | tf_op jit(solution)/shard_map/pallas_call | solution.py:342
  2.8 0.6 %collective-permute-start = (f32[40,256]{1,0:T(8,128)S(1)}, f32[40,256]{1,0:T(8,128)S(1)}, u32[]{:S(2)}, u32[]{:S(2)}) collective-permute-start(f32[40,256]{1,0:T(8,128)S(1)} %get-tuple-element.13), channel_id=1, source_target_pairs={{0,1},{1,0},{2,3},{3,2},{4,5},{5,4},{6,7},{7,6},{8,9},{9,8},{10,11... | collective-permute-start | bytes 122888 | tf_op jit(solution)/shard_map/ppermute | solution.py:281
  3.4 0.0 copy-done
  3.4 1.1 %copy.16 = bf16[80,4,128,8]{2,0,1,3:T(8,128)(2,1)} copy(bf16[80,4,128,8]{2,3,1,0:T(8,128)(2,1)S(1)} %copy-done) | data formatting | bytes 1310720 | tf_op args[0]
  4.5 0.0 collective-permute-done
  4.5 6.9 %all-to-all-start = ((bf16[8,4,80,128]{3,2,1,0:T(8,128)(2,1)}), bf16[8,4,80,128]{3,2,1,0:T(8,128)(2,1)S(1)}, u32[]{:S(2)}, u32[]{:S(2)}) async-start(bf16[8,4,80,128]{3,2,1,0:T(8,128)(2,1)} %bitcast.6), calls=%async_computation | async-start | bytes 1310720 | tf_op jit(solution)/shard_map/all_to_all | solution.py:297
  11.4 3.8 %collective-permute-start.1 = (f32[40,256]{1,0:T(8,128)S(1)}, f32[40,256]{1,0:T(8,128)S(1)}, u32[]{:S(2)}, u32[]{:S(2)}) collective-permute-start(f32[40,256]{1,0:T(8,128)S(1)} %add.27), channel_id=1, source_target_pairs={{0,24},{1,25},{2,26},{3,27},{4,28},{5,29},{6,30},{7,31},{8,16},{9,... | collective-permute-start | bytes 122888 | tf_op jit(solution)/shard_map/ppermute | solution.py:281
  15.2 0.0 collective-permute-start.2
  15.3 0.6 %collective-permute-start.3 = (f32[40,256]{1,0:T(8,128)S(1)}, f32[40,256]{1,0:T(8,128)S(1)}, u32[]{:S(2)}, u32[]{:S(2)}) collective-permute-start(f32[40,256]{1,0:T(8,128)S(1)} %add.27), channel_id=1, source_target_pairs={{0,8},{1,9},{2,10},{3,11},{4,12},{5,13},{6,14},{7,15},{8,0},{9,1},... | collective-permute-start | bytes 122888 | tf_op jit(solution)/shard_map/ppermute | solution.py:281
  15.8 12.6 %collective-permute-done.1 = f32[40,256]{1,0:T(8,128)S(1)} collective-permute-done((f32[40,256]{1,0:T(8,128)S(1)}, f32[40,256]{1,0:T(8,128)S(1)}, u32[]{:S(2)}, u32[]{:S(2)}) %collective-permute-start.1) | collective-permute-done | bytes 40992 | tf_op jit(solution)/shard_map/ppermute | solution.py:281
  28.4 4.4 %collective-permute-done.2 = f32[40,256]{1,0:T(8,128)S(1)} collective-permute-done((f32[40,256]{1,0:T(8,128)S(1)}, f32[40,256]{1,0:T(8,128)S(1)}, u32[]{:S(2)}, u32[]{:S(2)}) %collective-permute-start.2) | collective-permute-done | bytes 40992 | tf_op jit(solution)/shard_map/ppermute | solution.py:281
  32.8 0.0 collective-permute-done.3
  32.8 1.5 %collective-permute-start.4 = (f32[40,256]{1,0:T(8,128)S(1)}, f32[40,256]{1,0:T(8,128)S(1)}, u32[]{:S(2)}, u32[]{:S(2)}) collective-permute-start(f32[40,256]{1,0:T(8,128)S(1)} %add_add_fusion), channel_id=1, source_target_pairs={{0,4},{1,5},{2,6},{3,7},{4,0},{5,1},{6,2},{7,3},{8,12},{9,13},{10,... | collective-permute-start | bytes 122888 | tf_op jit(solution)/shard_map/ppermute | solution.py:281
  34.3 2.5 %collective-permute-done.4 = f32[40,256]{1,0:T(8,128)S(1)} collective-permute-done((f32[40,256]{1,0:T(8,128)S(1)}, f32[40,256]{1,0:T(8,128)S(1)}, u32[]{:S(2)}, u32[]{:S(2)}) %collective-permute-start.4) | collective-permute-done | bytes 40992 | tf_op jit(solution)/shard_map/ppermute | solution.py:281
  36.9 1.5 %collective-permute-start.5 = (f32[40,256]{1,0:T(8,128)S(1)}, f32[40,256]{1,0:T(8,128)S(1)}, u32[]{:S(2)}, u32[]{:S(2)}) collective-permute-start(f32[40,256]{1,0:T(8,128)S(1)} %add.31), channel_id=1, source_target_pairs={{0,2},{1,3},{2,0},{3,1},{4,6},{5,7},{6,4},{7,5},{8,10},{9,11},{10,... | collective-permute-start | bytes 122888 | tf_op jit(solution)/shard_map/ppermute | solution.py:281
  38.4 2.5 %collective-permute-done.5 = f32[40,256]{1,0:T(8,128)S(1)} collective-permute-done((f32[40,256]{1,0:T(8,128)S(1)}, f32[40,256]{1,0:T(8,128)S(1)}, u32[]{:S(2)}, u32[]{:S(2)}) %collective-permute-start.5) | collective-permute-done | bytes 40992 | tf_op jit(solution)/shard_map/ppermute | solution.py:281
  40.9 0.0 collective-permute-start.6
  40.9 1.2 %collective-permute-done.6.other_ref = f32[40,256]{1,0:T(8,128)S(1)} collective-permute-done((f32[40,256]{1,0:T(8,128)S(1)}, f32[40,256]{1,0:T(8,128)S(1)}, u32[]{:S(2)}, u32[]{:S(2)}) %collective-permute-start.6) | collective-permute-done | bytes 40992 | tf_op jit(solution)/shard_map/ppermute | solution.py:281
  42.1 11.7 %shard_map.101 = (bf16[80,128]{1,0:T(8,128)(2,1)S(1)}, bf16[80,128]{1,0:T(8,128)(2,1)S(1)}) custom-call(s32[1]{0:T(128)} %bitcast.own_ref, s32[1]{0:T(128)} %bitcast.1.half_ref, f32[40,256]{1,0:T(8,128)S(1)} %add.32.mine_ref, f32[40,256]{1,0:T(8,128)S(1)} %collective-permute-done.6.other_ref, f32[8,256]{1,0:T(8,128)S(1)} %get-tuple-element.15.aux_ref), custom_call_target="tpu_custom_call" | custom-call | flops 1000000000 | bytes 1000000 | tf_op jit(solution)/shard_map/pallas_call | solution.py:361
  53.8 0.0 all-to-all-done.whole_ref
  53.8 1.5 %shard_map.102 = bf16[80,4,1024]{2,1,0:T(4,128)(2,1)} custom-call(bf16[80,128]{1,0:T(8,128)(2,1)S(1)} %get-tuple-element.16.high_ref, bf16[80,128]{1,0:T(8,128)(2,1)S(1)} %get-tuple-element.17.low_ref, bf16[8,4,80,128]{3,2,1,0:T(8,128)(2,1)S(1)} %all-to-all-done.whole_ref), custom_call_target="tpu_custom_call" | custom-call | tf_op jit(solution)/shard_map/pallas_call | solution.py:378
  (4 shorter events, 0.0 us)
Async XLA Ops:
  0.0 3.4 %copy-start = (bf16[80,4,128,8]{2,3,1,0:T(8,128)(2,1)S(1)}, bf16[80,4,128,8]{2,3,1,0:T(8,128)(2,1)}, u32[]{:S(2)}) copy-start(bf16[80,4,128,8]{2,3,1,0:T(8,128)(2,1)} %param.10) | copy-start | bytes 1966084
  2.8 1.7 %collective-permute-start = (f32[40,256]{1,0:T(8,128)S(1)}, f32[40,256]{1,0:T(8,128)S(1)}, u32[]{:S(2)}, u32[]{:S(2)}) collective-permute-start(f32[40,256]{1,0:T(8,128)S(1)} %get-tuple-element.13), channel_id=1, source_target_pairs={{0,1},{1,0},{2,3},{3,2},{4,5},{5,4},{6,7},{7,6},{8,9},{9,8},{10,11... | collective-permute-start | bytes 122888 | tf_op jit(solution)/shard_map/ppermute | solution.py:281
  4.5 49.3 %all-to-all-start = ((bf16[8,4,80,128]{3,2,1,0:T(8,128)(2,1)}), bf16[8,4,80,128]{3,2,1,0:T(8,128)(2,1)S(1)}, u32[]{:S(2)}, u32[]{:S(2)}) async-start(bf16[8,4,80,128]{3,2,1,0:T(8,128)(2,1)} %bitcast.6), calls=%async_computation | async-start | bytes 1310720 | tf_op jit(solution)/shard_map/all_to_all | solution.py:297
  11.4 17.0 %collective-permute-start.1 = (f32[40,256]{1,0:T(8,128)S(1)}, f32[40,256]{1,0:T(8,128)S(1)}, u32[]{:S(2)}, u32[]{:S(2)}) collective-permute-start(f32[40,256]{1,0:T(8,128)S(1)} %add.27), channel_id=1, source_target_pairs={{0,24},{1,25},{2,26},{3,27},{4,28},{5,29},{6,30},{7,31},{8,16},{9,... | collective-permute-start | bytes 122888 | tf_op jit(solution)/shard_map/ppermute | solution.py:281
  15.2 17.6 %collective-permute-start.2 = (f32[40,256]{1,0:T(8,128)S(1)}, f32[40,256]{1,0:T(8,128)S(1)}, u32[]{:S(2)}, u32[]{:S(2)}) collective-permute-start(f32[40,256]{1,0:T(8,128)S(1)} %add.27), channel_id=1, source_target_pairs={{0,16},{1,17},{2,18},{3,19},{4,20},{5,21},{6,22},{7,23},{8,24},{9,... | collective-permute-start | bytes 122888 | tf_op jit(solution)/shard_map/ppermute | solution.py:281
  15.3 17.6 %collective-permute-start.3 = (f32[40,256]{1,0:T(8,128)S(1)}, f32[40,256]{1,0:T(8,128)S(1)}, u32[]{:S(2)}, u32[]{:S(2)}) collective-permute-start(f32[40,256]{1,0:T(8,128)S(1)} %add.27), channel_id=1, source_target_pairs={{0,8},{1,9},{2,10},{3,11},{4,12},{5,13},{6,14},{7,15},{8,0},{9,1},... | collective-permute-start | bytes 122888 | tf_op jit(solution)/shard_map/ppermute | solution.py:281
  32.8 4.1 %collective-permute-start.4 = (f32[40,256]{1,0:T(8,128)S(1)}, f32[40,256]{1,0:T(8,128)S(1)}, u32[]{:S(2)}, u32[]{:S(2)}) collective-permute-start(f32[40,256]{1,0:T(8,128)S(1)} %add_add_fusion), channel_id=1, source_target_pairs={{0,4},{1,5},{2,6},{3,7},{4,0},{5,1},{6,2},{7,3},{8,12},{9,13},{10,... | collective-permute-start | bytes 122888 | tf_op jit(solution)/shard_map/ppermute | solution.py:281
  36.9 4.0 %collective-permute-start.5 = (f32[40,256]{1,0:T(8,128)S(1)}, f32[40,256]{1,0:T(8,128)S(1)}, u32[]{:S(2)}, u32[]{:S(2)}) collective-permute-start(f32[40,256]{1,0:T(8,128)S(1)} %add.31), channel_id=1, source_target_pairs={{0,2},{1,3},{2,0},{3,1},{4,6},{5,7},{6,4},{7,5},{8,10},{9,11},{10,... | collective-permute-start | bytes 122888 | tf_op jit(solution)/shard_map/ppermute | solution.py:281
  40.9 1.2 %collective-permute-start.6 = (f32[40,256]{1,0:T(8,128)S(1)}, f32[40,256]{1,0:T(8,128)S(1)}, u32[]{:S(2)}, u32[]{:S(2)}) collective-permute-start(f32[40,256]{1,0:T(8,128)S(1)} %add.32.mine_ref), channel_id=1, source_target_pairs={{0,1},{1,0},{2,3},{3,2},{4,5},{5,4},{6,7},{7,6},{8,9},{9,8},{10,11... | collective-permute-start | bytes 122888 | tf_op jit(solution)/shard_map/ppermute | solution.py:281

commit v5 on v4

--- a/solution.py
+++ b/solution.py
@@ -45,8 +45,8 @@
 
 
 def prior_kernel(first_ref, half_ref, *refs):
-    inputs, (keep_ref, send_ref, aux_ref), held, arrived = (
-        refs[:11], refs[11:14], refs[14:25], refs[25]
+    inputs, (keep_ref, send_ref, aux_ref), held, arrived, grid_ref = (
+        refs[:11], refs[11:14], refs[14:25], refs[25], refs[26]
     )
     copies = [
         pltpu.make_async_copy(source, target, arrived.at[i])
@@ -102,17 +102,44 @@
     inside = (row // STRIDE == spot_row) & (col // STRIDE == spot_col)
     place = jnp.where(inside, weight, 0.0)
 
+    weights = [place * heights[level : level + 1] for level in range(levels)]
     copies[-1].wait()
-    total = jnp.zeros((members * regions, count), f32)
-    for level in range(levels):
-        grid = state_ref[:, level].astype(f32).reshape(members * regions, pixels).astype(bf16)
-        for piece in split3(place * heights[level : level + 1]):
-            total = total + dot(grid, piece, 1, 0, None)
-    home = jnp.zeros((1, count), jnp.int32)
-    for k in range(batches):
-        home = jnp.where(lane // size == k, home_ref[k], home)
-    here = iota((regions, count), 0) == home
-    share = jnp.sum(jnp.where(here[None], total.reshape(members, regions, count), 0.0), axis=1)
+    if pixels == LANES and LANES % size == 0 and count % LANES == 0:
+        for level in range(levels):
+            grid_ref[level] = state_ref[:, level].astype(f32).reshape(members * regions, pixels)
+        together = LANES // size
+        tiles = []
+        for tile in range(count // LANES):
+            heavy = jnp.concatenate(
+                [w[:, LANES * tile : LANES * tile + LANES] for w in weights], axis=0
+            )
+            high = heavy.astype(bf16)
+            low = (heavy - high.astype(f32)).astype(bf16)
+            rows = []
+            for k in range(tile * together, (tile + 1) * together):
+                pick = pl.ds(home_ref[k], members, stride=regions)
+                parts = [grid_ref[level, pick, :].astype(bf16) for level in range(levels)]
+                rows.append(jnp.concatenate(parts, axis=1))
+            grid = jnp.concatenate(rows, axis=0)
+            value = dot(grid, high, 1, 0, None) + dot(grid, low, 1, 0, None)
+            best = value[:members]
+            for i in range(1, together):
+                mine = iota((1, LANES), 1) // size == i
+                best = jnp.where(mine, value[members * i : members * i + members], best)
+            tiles.append(best)
+        share = jnp.concatenate(tiles, axis=1)
+    else:
+        total = jnp.zeros((members * regions, count), f32)
+        for level in range(levels):
+            grid = state_ref[:, level].astype(f32).reshape(members * regions, pixels)
+            for piece in split3(weights[level]):
+                total = total + dot(grid.astype(bf16), piece, 1, 0, None)
+        home = jnp.zeros((1, count), jnp.int32)
+        for k in range(batches):
+            home = jnp.where(lane // size == k, home_ref[k], home)
+        here = iota((regions, count), 0) == home
+        total = total.reshape(members, regions, count)
+        share = jnp.sum(jnp.where(here[None], total, 0.0), axis=1)
     half = keep_ref.shape[0]
     if 2 * half > members:
         share = jnp.concatenate([share, jnp.zeros((2 * half - members, count), f32)], axis=0)
@@ -260,18 +287,30 @@
     low_ref[...] = (mixing - high.astype(f32)).astype(bf16)
 
 
-def apply_kernel(high_ref, low_ref, whole_ref, out_ref, row_ref):
+def apply_kernel(high_ref, low_ref, whole_ref, out_ref, row_ref, stage_ref, sent):
     sources, levels, members, pixels = whole_ref.shape
     high, low = high_ref[:, :members], low_ref[:, :members]
-    for level in range(levels):
-        field = jnp.concatenate([whole_ref[s, level] for s in range(sources)], axis=1)
-        value = dot(high, field, 0, 0, None) + dot(low, field, 0, 0, None)
-        for s in range(sources):
-            part = value[:, pixels * s : pixels * s + pixels]
-            row_ref[s, pl.ds(level, members, stride=levels), :] = part
-    for s in range(sources):
-        part = row_ref[s].reshape(members, levels, pixels).astype(bf16)
-        out_ref[:, :, pixels * s : pixels * s + pixels] = part
+    parts = sent.shape[0]
+    each = sources // parts
+    copies = []
+    for part in range(parts):
+        group = range(part * each, part * each + each)
+        for level in range(levels):
+            field = jnp.concatenate([whole_ref[s, level] for s in group], axis=1)
+            value = dot(high, field, 0, 0, None) + dot(low, field, 0, 0, None)
+            for i, s in enumerate(group):
+                piece = value[:, pixels * i : pixels * i + pixels]
+                row_ref[s, pl.ds(level, members, stride=levels), :] = piece
+        for s in group:
+            piece = row_ref[s].reshape(members, levels, pixels).astype(bf16)
+            stage_ref[:, :, pixels * s : pixels * s + pixels] = piece
+        span = pl.ds(part * each * pixels, each * pixels)
+        copies.append(
+            pltpu.make_async_copy(stage_ref.at[:, :, span], out_ref.at[:, :, span], sent.at[part])
+        )
+        copies[-1].start()
+    for copy in copies:
+        copy.wait()
 
 
 BOTH = ("region", "lev")
@@ -350,7 +389,10 @@
         out_specs=(vmem, vmem, vmem),
         scratch_shapes=[pltpu.SMEM(x.shape, x.dtype) for x in scalars]
         + [pltpu.VMEM(x.shape, x.dtype) for x in tables]
-        + [pltpu.SemaphoreType.DMA((11,))],
+        + [
+            pltpu.SemaphoreType.DMA((11,)),
+            pltpu.VMEM((levels, members * local.shape[2], pixels), f32),
+        ],
         compiler_params=pltpu.CompilerParams(vmem_limit_bytes=24 * 2**20),
     )(
         (own_region * pixels)[None],
@@ -379,8 +421,12 @@
             apply_kernel,
             out_shape=jax.ShapeDtypeStruct((members, levels, pixels * region_count), bf16),
             in_specs=[vmem] * 3,
-            out_specs=vmem,
-            scratch_shapes=[pltpu.VMEM((region_count, members * levels, pixels), f32)],
+            out_specs=pl.BlockSpec(memory_space=pltpu.HBM),
+            scratch_shapes=[
+                pltpu.VMEM((region_count, members * levels, pixels), f32),
+                pltpu.VMEM((members, levels, pixels * region_count), bf16),
+                pltpu.SemaphoreType.DMA((2 if region_count % 2 == 0 else 1,)),
+            ],
             compiler_params=pltpu.CompilerParams(vmem_limit_bytes=24 * 2**20),
         )(*pieces, whole)
         return result[:, :, None]

time: 55.6 us -> 54.6 us (0.982)
  Pallas kernels: 16 us -> 15.1 us
    pallas_call x1, Pallas kernels: 2.81 us -> 2.04 us  [body(): pl.pallas_call(prior_kernel, out_shape=(jax.ShapeDtypeStruct((half, count...]
where the time goes in v5:
time: 54.6 us; the launch traced here: 54.4 us
  waiting for transfers between devices  23.2 us (42%)
  Pallas kernels  15.1 us (28%)
  starting transfers between devices  14.9 us (27%)
  local copies, waits for them, and re-layouts  1.09 us (2%)
    ppermute x7, waiting for transfers between devices, swap(): return lax.ppermute(x, BOTH, [(i, i ^ k) for i in range(devices)])  23.2 us
    pallas_call x1, Pallas kernels, body(): pl.pallas_call(functools.partial(filter_kernel, members, batches), out_sh...  11.7 us
    ppermute x7, starting transfers between devices, swap(): return lax.ppermute(x, BOTH, [(i, i ^ k) for i in range(devices)])  7.99 us
    all_to_all x1, starting transfers between devices, exchange(): lax.all_to_all(state, 'region', split_axis=0, concat_axis=0, tiled=True)  6.94 us
    pallas_call x1, Pallas kernels, body(): pl.pallas_call(prior_kernel, out_shape=(jax.ShapeDtypeStruct((half, count...  2.04 us
    pallas_call x1, Pallas kernels, body(): pl.pallas_call(apply_kernel, out_shape=jax.ShapeDtypeStruct((members, lev...  1.38 us
    unnamed x3, local copies, waits for them, and re-layouts  1.09 us
  transfers between devices with their start and end apart: 8, of which 5 were waited for; matrix products, arithmetic and copies ran while one was open for 2% of the time, Pallas kernels for 21%

profile of v5, /device:TPU:0, one launch (start us, length us, event | category | flops | bytes accessed | tf_op | source)
XLA Modules:
  0.0 54.4 jit_solution(13968823835027190523)
XLA Ops:
  0.0 0.0 copy-start
  0.0 2.0 %shard_map.100 = (f32[40,256]{1,0:T(8,128)S(1)}, f32[40,256]{1,0:T(8,128)S(1)}, f32[8,256]{1,0:T(8,128)S(1)}) custom-call(s32[1]{0:T(128)} %bitcast.2.first_ref, s32[1]{0:T(128)} %bitcast.1.half_ref, f32[4]{0:T(128)} %refs_0_.1, f32[4]{0:T(128)} %refs_1_.1, s32[4]{0:T(128)} %refs_3_.1, s32[4]{0:T(128)} %refs_3_.1, s32[8]{0:T(128)} %refs_4_.1, ...), custom_call_target="tpu_custom_call" | custom-call | tf_op jit(solution)/shard_map/pallas_call | solution.py:381
  2.1 0.6 %collective-permute-start = (f32[40,256]{1,0:T(8,128)S(1)}, f32[40,256]{1,0:T(8,128)S(1)}, u32[]{:S(2)}, u32[]{:S(2)}) collective-permute-start(f32[40,256]{1,0:T(8,128)S(1)} %get-tuple-element.13), channel_id=1, source_target_pairs={{0,1},{1,0},{2,3},{3,2},{4,5},{5,4},{6,7},{7,6},{8,9},{9,8},{10,11... | collective-permute-start | bytes 122888 | tf_op jit(solution)/shard_map/ppermute | solution.py:320
  2.6 0.0 copy-done
  2.6 1.1 %copy.16 = bf16[80,4,128,8]{2,0,1,3:T(8,128)(2,1)} copy(bf16[80,4,128,8]{2,3,1,0:T(8,128)(2,1)S(1)} %copy-done) | data formatting | bytes 1310720 | tf_op args[0]
  3.7 0.0 collective-permute-done
  3.7 6.9 %all-to-all-start = ((bf16[8,4,80,128]{3,2,1,0:T(8,128)(2,1)}), bf16[8,4,80,128]{3,2,1,0:T(8,128)(2,1)S(1)}, u32[]{:S(2)}, u32[]{:S(2)}) async-start(bf16[8,4,80,128]{3,2,1,0:T(8,128)(2,1)} %bitcast.6), calls=%async_computation | async-start | bytes 1310720 | tf_op jit(solution)/shard_map/all_to_all | solution.py:336
  10.7 3.8 %collective-permute-start.1 = (f32[40,256]{1,0:T(8,128)S(1)}, f32[40,256]{1,0:T(8,128)S(1)}, u32[]{:S(2)}, u32[]{:S(2)}) collective-permute-start(f32[40,256]{1,0:T(8,128)S(1)} %add.27), channel_id=1, source_target_pairs={{0,24},{1,25},{2,26},{3,27},{4,28},{5,29},{6,30},{7,31},{8,16},{9,... | collective-permute-start | bytes 122888 | tf_op jit(solution)/shard_map/ppermute | solution.py:320
  14.5 0.0 collective-permute-start.2
  14.5 0.6 %collective-permute-start.3 = (f32[40,256]{1,0:T(8,128)S(1)}, f32[40,256]{1,0:T(8,128)S(1)}, u32[]{:S(2)}, u32[]{:S(2)}) collective-permute-start(f32[40,256]{1,0:T(8,128)S(1)} %add.27), channel_id=1, source_target_pairs={{0,8},{1,9},{2,10},{3,11},{4,12},{5,13},{6,14},{7,15},{8,0},{9,1},... | collective-permute-start | bytes 122888 | tf_op jit(solution)/shard_map/ppermute | solution.py:320
  15.1 12.6 %collective-permute-done.1 = f32[40,256]{1,0:T(8,128)S(1)} collective-permute-done((f32[40,256]{1,0:T(8,128)S(1)}, f32[40,256]{1,0:T(8,128)S(1)}, u32[]{:S(2)}, u32[]{:S(2)}) %collective-permute-start.1) | collective-permute-done | bytes 40992 | tf_op jit(solution)/shard_map/ppermute | solution.py:320
  27.6 4.4 %collective-permute-done.2 = f32[40,256]{1,0:T(8,128)S(1)} collective-permute-done((f32[40,256]{1,0:T(8,128)S(1)}, f32[40,256]{1,0:T(8,128)S(1)}, u32[]{:S(2)}, u32[]{:S(2)}) %collective-permute-start.2) | collective-permute-done | bytes 40992 | tf_op jit(solution)/shard_map/ppermute | solution.py:320
  32.0 0.0 collective-permute-done.3
  32.0 1.5 %collective-permute-start.4 = (f32[40,256]{1,0:T(8,128)S(1)}, f32[40,256]{1,0:T(8,128)S(1)}, u32[]{:S(2)}, u32[]{:S(2)}) collective-permute-start(f32[40,256]{1,0:T(8,128)S(1)} %add_add_fusion), channel_id=1, source_target_pairs={{0,4},{1,5},{2,6},{3,7},{4,0},{5,1},{6,2},{7,3},{8,12},{9,13},{10,... | collective-permute-start | bytes 122888 | tf_op jit(solution)/shard_map/ppermute | solution.py:320
  33.6 2.5 %collective-permute-done.4 = f32[40,256]{1,0:T(8,128)S(1)} collective-permute-done((f32[40,256]{1,0:T(8,128)S(1)}, f32[40,256]{1,0:T(8,128)S(1)}, u32[]{:S(2)}, u32[]{:S(2)}) %collective-permute-start.4) | collective-permute-done | bytes 40992 | tf_op jit(solution)/shard_map/ppermute | solution.py:320
  36.1 1.5 %collective-permute-start.5 = (f32[40,256]{1,0:T(8,128)S(1)}, f32[40,256]{1,0:T(8,128)S(1)}, u32[]{:S(2)}, u32[]{:S(2)}) collective-permute-start(f32[40,256]{1,0:T(8,128)S(1)} %add.31), channel_id=1, source_target_pairs={{0,2},{1,3},{2,0},{3,1},{4,6},{5,7},{6,4},{7,5},{8,10},{9,11},{10,... | collective-permute-start | bytes 122888 | tf_op jit(solution)/shard_map/ppermute | solution.py:320
  37.6 2.5 %collective-permute-done.5 = f32[40,256]{1,0:T(8,128)S(1)} collective-permute-done((f32[40,256]{1,0:T(8,128)S(1)}, f32[40,256]{1,0:T(8,128)S(1)}, u32[]{:S(2)}, u32[]{:S(2)}) %collective-permute-start.5) | collective-permute-done | bytes 40992 | tf_op jit(solution)/shard_map/ppermute | solution.py:320
  40.1 0.0 collective-permute-start.6
  40.1 1.2 %collective-permute-done.6.other_ref = f32[40,256]{1,0:T(8,128)S(1)} collective-permute-done((f32[40,256]{1,0:T(8,128)S(1)}, f32[40,256]{1,0:T(8,128)S(1)}, u32[]{:S(2)}, u32[]{:S(2)}) %collective-permute-start.6) | collective-permute-done | bytes 40992 | tf_op jit(solution)/shard_map/ppermute | solution.py:320
  41.4 11.7 %shard_map.101 = (bf16[80,128]{1,0:T(8,128)(2,1)S(1)}, bf16[80,128]{1,0:T(8,128)(2,1)S(1)}) custom-call(s32[1]{0:T(128)} %bitcast.own_ref, s32[1]{0:T(128)} %bitcast.1.half_ref, f32[40,256]{1,0:T(8,128)S(1)} %add.32.mine_ref, f32[40,256]{1,0:T(8,128)S(1)} %collective-permute-done.6.other_ref, f32[8,256]{1,0:T(8,128)S(1)} %get-tuple-element.15.aux_ref), custom_call_target="tpu_custom_call" | custom-call | flops 1000000000 | bytes 1000000 | tf_op jit(solution)/shard_map/pallas_call | solution.py:403
  53.1 0.0 all-to-all-done.whole_ref
  53.1 1.4 %shard_map.102 = bf16[80,4,1024]{2,1,0:T(4,128)(2,1)} custom-call(bf16[80,128]{1,0:T(8,128)(2,1)S(1)} %get-tuple-element.16.high_ref, bf16[80,128]{1,0:T(8,128)(2,1)S(1)} %get-tuple-element.17.low_ref, bf16[8,4,80,128]{3,2,1,0:T(8,128)(2,1)S(1)} %all-to-all-done.whole_ref), custom_call_target="tpu_custom_call" | custom-call | tf_op jit(solution)/shard_map/pallas_call | solution.py:420
  (4 shorter events, 0.0 us)
Async XLA Ops:
  0.0 2.6 %copy-start = (bf16[80,4,128,8]{2,3,1,0:T(8,128)(2,1)S(1)}, bf16[80,4,128,8]{2,3,1,0:T(8,128)(2,1)}, u32[]{:S(2)}) copy-start(bf16[80,4,128,8]{2,3,1,0:T(8,128)(2,1)} %param.10) | copy-start | bytes 1966084
  2.1 1.7 %collective-permute-start = (f32[40,256]{1,0:T(8,128)S(1)}, f32[40,256]{1,0:T(8,128)S(1)}, u32[]{:S(2)}, u32[]{:S(2)}) collective-permute-start(f32[40,256]{1,0:T(8,128)S(1)} %get-tuple-element.13), channel_id=1, source_target_pairs={{0,1},{1,0},{2,3},{3,2},{4,5},{5,4},{6,7},{7,6},{8,9},{9,8},{10,11... | collective-permute-start | bytes 122888 | tf_op jit(solution)/shard_map/ppermute | solution.py:320
  3.7 49.3 %all-to-all-start = ((bf16[8,4,80,128]{3,2,1,0:T(8,128)(2,1)}), bf16[8,4,80,128]{3,2,1,0:T(8,128)(2,1)S(1)}, u32[]{:S(2)}, u32[]{:S(2)}) async-start(bf16[8,4,80,128]{3,2,1,0:T(8,128)(2,1)} %bitcast.6), calls=%async_computation | async-start | bytes 1310720 | tf_op jit(solution)/shard_map/all_to_all | solution.py:336
  10.7 17.0 %collective-permute-start.1 = (f32[40,256]{1,0:T(8,128)S(1)}, f32[40,256]{1,0:T(8,128)S(1)}, u32[]{:S(2)}, u32[]{:S(2)}) collective-permute-start(f32[40,256]{1,0:T(8,128)S(1)} %add.27), channel_id=1, source_target_pairs={{0,24},{1,25},{2,26},{3,27},{4,28},{5,29},{6,30},{7,31},{8,16},{9,... | collective-permute-start | bytes 122888 | tf_op jit(solution)/shard_map/ppermute | solution.py:320
  14.5 17.6 %collective-permute-start.2 = (f32[40,256]{1,0:T(8,128)S(1)}, f32[40,256]{1,0:T(8,128)S(1)}, u32[]{:S(2)}, u32[]{:S(2)}) collective-permute-start(f32[40,256]{1,0:T(8,128)S(1)} %add.27), channel_id=1, source_target_pairs={{0,16},{1,17},{2,18},{3,19},{4,20},{5,21},{6,22},{7,23},{8,24},{9,... | collective-permute-start | bytes 122888 | tf_op jit(solution)/shard_map/ppermute | solution.py:320
  14.5 17.6 %collective-permute-start.3 = (f32[40,256]{1,0:T(8,128)S(1)}, f32[40,256]{1,0:T(8,128)S(1)}, u32[]{:S(2)}, u32[]{:S(2)}) collective-permute-start(f32[40,256]{1,0:T(8,128)S(1)} %add.27), channel_id=1, source_target_pairs={{0,8},{1,9},{2,10},{3,11},{4,12},{5,13},{6,14},{7,15},{8,0},{9,1},... | collective-permute-start | bytes 122888 | tf_op jit(solution)/shard_map/ppermute | solution.py:320
  32.0 4.1 %collective-permute-start.4 = (f32[40,256]{1,0:T(8,128)S(1)}, f32[40,256]{1,0:T(8,128)S(1)}, u32[]{:S(2)}, u32[]{:S(2)}) collective-permute-start(f32[40,256]{1,0:T(8,128)S(1)} %add_add_fusion), channel_id=1, source_target_pairs={{0,4},{1,5},{2,6},{3,7},{4,0},{5,1},{6,2},{7,3},{8,12},{9,13},{10,... | collective-permute-start | bytes 122888 | tf_op jit(solution)/shard_map/ppermute | solution.py:320
  36.1 4.0 %collective-permute-start.5 = (f32[40,256]{1,0:T(8,128)S(1)}, f32[40,256]{1,0:T(8,128)S(1)}, u32[]{:S(2)}, u32[]{:S(2)}) collective-permute-start(f32[40,256]{1,0:T(8,128)S(1)} %add.31), channel_id=1, source_target_pairs={{0,2},{1,3},{2,0},{3,1},{4,6},{5,7},{6,4},{7,5},{8,10},{9,11},{10,... | collective-permute-start | bytes 122888 | tf_op jit(solution)/shard_map/ppermute | solution.py:320
  40.1 1.2 %collective-permute-start.6 = (f32[40,256]{1,0:T(8,128)S(1)}, f32[40,256]{1,0:T(8,128)S(1)}, u32[]{:S(2)}, u32[]{:S(2)}) collective-permute-start(f32[40,256]{1,0:T(8,128)S(1)} %add.32.mine_ref), channel_id=1, source_target_pairs={{0,1},{1,0},{2,3},{3,2},{4,5},{5,4},{6,7},{7,6},{8,9},{9,8},{10,11... | collective-permute-start | bytes 122888 | tf_op jit(solution)/shard_map/ppermute | solution.py:320

commit v6 on v5

--- a/solution.py
+++ b/solution.py
@@ -72,7 +72,15 @@
     hit = order == iota((size, count), 0)
     rows = []
     for ref in (place_ref, amount_ref, noise_ref):
-        wide = dot(ref[...].astype(f32), spread, 0, 0)
+        if ref is place_ref and batches <= SUB and size <= LANES:
+            square = jnp.concatenate([ref[...].astype(f32)] + [jnp.zeros((1, size), f32)] * (SUB - batches), axis=0)
+            square = jnp.concatenate([square, jnp.zeros((SUB, LANES - size), f32)], axis=1)
+            upright = square.T
+            wide = jnp.zeros((size, count), f32)
+            for k in range(batches):
+                wide = jnp.where(lane // size == k, upright[:size, k : k + 1], wide)
+        else:
+            wide = dot(ref[...].astype(f32), spread, 0, 0)
         rows.append(jnp.sum(jnp.where(hit, wide, 0.0), axis=0, keepdims=True))
     picked = rows[0].astype(jnp.int32)
     channel = picked // sites
@@ -87,8 +95,9 @@
     spot = picked - channel * sites
     spot_row = spot // (TILE // STRIDE)
     spot_col = spot - spot_row * (TILE // STRIDE)
-    chosen = jnp.where(iota((channels, count), 0) == channel, 1.0, 0.0).astype(f32)
-    heights = dot(height_ref[...], chosen, 1, 0)
+    heights = jnp.zeros((levels, count), f32)
+    for c in range(channels):
+        heights = jnp.where(channel == c, height_ref[:, c : c + 1], heights)
 
     pixel = iota((pixels, 1), 0) + first_ref[0]
     row = pixel // TILE
@@ -327,7 +336,7 @@
     stages = []
     bit = 8
     while bit < devices:
-        stages.append((3 * bit, 2 * bit, bit) if 2 * bit < devices else (bit,))
+        stages.append((3 * bit, bit, 2 * bit) if 2 * bit < devices else (bit,))
         bit *= 4
     stages += [(k,) for k in (4, 2) if k < devices]
     for steps in stages:
@@ -425,7 +434,7 @@
             scratch_shapes=[
                 pltpu.VMEM((region_count, members * levels, pixels), f32),
                 pltpu.VMEM((members, levels, pixels * region_count), bf16),
-                pltpu.SemaphoreType.DMA((2 if region_count % 2 == 0 else 1,)),
+                pltpu.SemaphoreType.DMA((4 if region_count % 4 == 0 else 1,)),
             ],
             compiler_params=pltpu.CompilerParams(vmem_limit_bytes=24 * 2**20),
         )(*pieces, whole)

time: 54.6 us -> 54.4 us (level)
  transfers between devices with their start and end apart: 8 -> 8, of which waited for: 5 -> 5; matrix products, arithmetic and copies ran while one was open for 2% -> 2% of each run, Pallas kernels for 21% -> 22%
where the time goes in v6:
time: 54.4 us; the launch traced here: 54.2 us
  waiting for transfers between devices  23.2 us (43%)
  starting transfers between devices  14.9 us (27%)
  Pallas kernels  14.8 us (27%)
  local copies, waits for them, and re-layouts  1.09 us (2%)
    ppermute x7, waiting for transfers between devices, swap(): return lax.ppermute(x, BOTH, [(i, i ^ k) for i in range(devices)])  23.2 us
    pallas_call x1, Pallas kernels, body(): pl.pallas_call(functools.partial(filter_kernel, members, batches), out_sh...  11.7 us
    ppermute x7, starting transfers between devices, swap(): return lax.ppermute(x, BOTH, [(i, i ^ k) for i in range(devices)])  7.99 us
    all_to_all x1, starting transfers between devices, exchange(): lax.all_to_all(state, 'region', split_axis=0, concat_axis=0, tiled=True)  6.94 us
    pallas_call x1, Pallas kernels, body(): pl.pallas_call(prior_kernel, out_shape=(jax.ShapeDtypeStruct((half, count...  1.85 us
    pallas_call x1, Pallas kernels, body(): pl.pallas_call(apply_kernel, out_shape=jax.ShapeDtypeStruct((members, lev...  1.3 us
    unnamed x3, local copies, waits for them, and re-layouts  1.09 us
  transfers between devices with their start and end apart: 8, of which 5 were waited for; matrix products, arithmetic and copies ran while one was open for 2% of the time, Pallas kernels for 22%

profile of v6, /device:TPU:0, one launch (start us, length us, event | category | flops | bytes accessed | tf_op | source)
XLA Modules:
  0.0 54.2 jit_solution(7459255999444600658)
XLA Ops:
  0.0 0.0 copy-start
  0.0 1.9 %shard_map.100 = (f32[40,256]{1,0:T(8,128)S(1)}, f32[40,256]{1,0:T(8,128)S(1)}, f32[8,256]{1,0:T(8,128)S(1)}) custom-call(s32[1]{0:T(128)} %bitcast.2.first_ref, s32[1]{0:T(128)} %bitcast.1.half_ref, f32[4]{0:T(128)} %refs_0_.1, f32[4]{0:T(128)} %refs_1_.1, s32[4]{0:T(128)} %refs_3_.1, s32[4]{0:T(128)} %refs_3_.1, s32[8]{0:T(128)} %refs_4_.1, ...), custom_call_target="tpu_custom_call" | custom-call | tf_op jit(solution)/shard_map/pallas_call | solution.py:390
  1.9 0.6 %collective-permute-start = (f32[40,256]{1,0:T(8,128)S(1)}, f32[40,256]{1,0:T(8,128)S(1)}, u32[]{:S(2)}, u32[]{:S(2)}) collective-permute-start(f32[40,256]{1,0:T(8,128)S(1)} %get-tuple-element.13), channel_id=1, source_target_pairs={{0,1},{1,0},{2,3},{3,2},{4,5},{5,4},{6,7},{7,6},{8,9},{9,8},{10,11... | collective-permute-start | bytes 122888 | tf_op jit(solution)/shard_map/ppermute | solution.py:329
  2.4 0.0 copy-done
  2.4 1.1 %copy.16 = bf16[80,4,128,8]{2,0,1,3:T(8,128)(2,1)} copy(bf16[80,4,128,8]{2,3,1,0:T(8,128)(2,1)S(1)} %copy-done) | data formatting | bytes 1310720 | tf_op args[0]
  3.5 0.0 collective-permute-done
  3.5 6.9 %all-to-all-start = ((bf16[8,4,80,128]{3,2,1,0:T(8,128)(2,1)}), bf16[8,4,80,128]{3,2,1,0:T(8,128)(2,1)S(1)}, u32[]{:S(2)}, u32[]{:S(2)}) async-start(bf16[8,4,80,128]{3,2,1,0:T(8,128)(2,1)} %bitcast.6), calls=%async_computation | async-start | bytes 1310720 | tf_op jit(solution)/shard_map/all_to_all | solution.py:345
  10.5 3.8 %collective-permute-start.1 = (f32[40,256]{1,0:T(8,128)S(1)}, f32[40,256]{1,0:T(8,128)S(1)}, u32[]{:S(2)}, u32[]{:S(2)}) collective-permute-start(f32[40,256]{1,0:T(8,128)S(1)} %add.27), channel_id=1, source_target_pairs={{0,24},{1,25},{2,26},{3,27},{4,28},{5,29},{6,30},{7,31},{8,16},{9,... | collective-permute-start | bytes 122888 | tf_op jit(solution)/shard_map/ppermute | solution.py:329
  14.3 0.0 collective-permute-start.2
  14.3 0.6 %collective-permute-start.3 = (f32[40,256]{1,0:T(8,128)S(1)}, f32[40,256]{1,0:T(8,128)S(1)}, u32[]{:S(2)}, u32[]{:S(2)}) collective-permute-start(f32[40,256]{1,0:T(8,128)S(1)} %add.27), channel_id=1, source_target_pairs={{0,16},{1,17},{2,18},{3,19},{4,20},{5,21},{6,22},{7,23},{8,24},{9,... | collective-permute-start | bytes 122888 | tf_op jit(solution)/shard_map/ppermute | solution.py:329
  14.9 12.6 %collective-permute-done.1 = f32[40,256]{1,0:T(8,128)S(1)} collective-permute-done((f32[40,256]{1,0:T(8,128)S(1)}, f32[40,256]{1,0:T(8,128)S(1)}, u32[]{:S(2)}, u32[]{:S(2)}) %collective-permute-start.1) | collective-permute-done | bytes 40992 | tf_op jit(solution)/shard_map/ppermute | solution.py:329
  27.4 0.0 collective-permute-done.2
  27.4 4.4 %collective-permute-done.3 = f32[40,256]{1,0:T(8,128)S(1)} collective-permute-done((f32[40,256]{1,0:T(8,128)S(1)}, f32[40,256]{1,0:T(8,128)S(1)}, u32[]{:S(2)}, u32[]{:S(2)}) %collective-permute-start.3) | collective-permute-done | bytes 40992 | tf_op jit(solution)/shard_map/ppermute | solution.py:329
  31.9 1.5 %collective-permute-start.4 = (f32[40,256]{1,0:T(8,128)S(1)}, f32[40,256]{1,0:T(8,128)S(1)}, u32[]{:S(2)}, u32[]{:S(2)}) collective-permute-start(f32[40,256]{1,0:T(8,128)S(1)} %add_add_fusion), channel_id=1, source_target_pairs={{0,4},{1,5},{2,6},{3,7},{4,0},{5,1},{6,2},{7,3},{8,12},{9,13},{10,... | collective-permute-start | bytes 122888 | tf_op jit(solution)/shard_map/ppermute | solution.py:329
  33.4 2.5 %collective-permute-done.4 = f32[40,256]{1,0:T(8,128)S(1)} collective-permute-done((f32[40,256]{1,0:T(8,128)S(1)}, f32[40,256]{1,0:T(8,128)S(1)}, u32[]{:S(2)}, u32[]{:S(2)}) %collective-permute-start.4) | collective-permute-done | bytes 40992 | tf_op jit(solution)/shard_map/ppermute | solution.py:329
  35.9 1.5 %collective-permute-start.5 = (f32[40,256]{1,0:T(8,128)S(1)}, f32[40,256]{1,0:T(8,128)S(1)}, u32[]{:S(2)}, u32[]{:S(2)}) collective-permute-start(f32[40,256]{1,0:T(8,128)S(1)} %add.31), channel_id=1, source_target_pairs={{0,2},{1,3},{2,0},{3,1},{4,6},{5,7},{6,4},{7,5},{8,10},{9,11},{10,... | collective-permute-start | bytes 122888 | tf_op jit(solution)/shard_map/ppermute | solution.py:329
  37.4 2.5 %collective-permute-done.5 = f32[40,256]{1,0:T(8,128)S(1)} collective-permute-done((f32[40,256]{1,0:T(8,128)S(1)}, f32[40,256]{1,0:T(8,128)S(1)}, u32[]{:S(2)}, u32[]{:S(2)}) %collective-permute-start.5) | collective-permute-done | bytes 40992 | tf_op jit(solution)/shard_map/ppermute | solution.py:329
  39.9 0.0 collective-permute-start.6
  39.9 1.2 %collective-permute-done.6.other_ref = f32[40,256]{1,0:T(8,128)S(1)} collective-permute-done((f32[40,256]{1,0:T(8,128)S(1)}, f32[40,256]{1,0:T(8,128)S(1)}, u32[]{:S(2)}, u32[]{:S(2)}) %collective-permute-start.6) | collective-permute-done | bytes 40992 | tf_op jit(solution)/shard_map/ppermute | solution.py:329
  41.2 11.7 %shard_map.101 = (bf16[80,128]{1,0:T(8,128)(2,1)S(1)}, bf16[80,128]{1,0:T(8,128)(2,1)S(1)}) custom-call(s32[1]{0:T(128)} %bitcast.own_ref, s32[1]{0:T(128)} %bitcast.1.half_ref, f32[40,256]{1,0:T(8,128)S(1)} %add.32.mine_ref, f32[40,256]{1,0:T(8,128)S(1)} %collective-permute-done.6.other_ref, f32[8,256]{1,0:T(8,128)S(1)} %get-tuple-element.15.aux_ref), custom_call_target="tpu_custom_call" | custom-call | flops 1000000000 | bytes 1000000 | tf_op jit(solution)/shard_map/pallas_call | solution.py:412
  52.9 0.0 all-to-all-done.whole_ref
  52.9 1.3 %shard_map.102 = bf16[80,4,1024]{2,1,0:T(4,128)(2,1)} custom-call(bf16[80,128]{1,0:T(8,128)(2,1)S(1)} %get-tuple-element.16.high_ref, bf16[80,128]{1,0:T(8,128)(2,1)S(1)} %get-tuple-element.17.low_ref, bf16[8,4,80,128]{3,2,1,0:T(8,128)(2,1)S(1)} %all-to-all-done.whole_ref), custom_call_target="tpu_custom_call" | custom-call | tf_op jit(solution)/shard_map/pallas_call | solution.py:429
  (4 shorter events, 0.0 us)
Async XLA Ops:
  0.0 2.4 %copy-start = (bf16[80,4,128,8]{2,3,1,0:T(8,128)(2,1)S(1)}, bf16[80,4,128,8]{2,3,1,0:T(8,128)(2,1)}, u32[]{:S(2)}) copy-start(bf16[80,4,128,8]{2,3,1,0:T(8,128)(2,1)} %param.10) | copy-start | bytes 1966084
  1.9 1.7 %collective-permute-start = (f32[40,256]{1,0:T(8,128)S(1)}, f32[40,256]{1,0:T(8,128)S(1)}, u32[]{:S(2)}, u32[]{:S(2)}) collective-permute-start(f32[40,256]{1,0:T(8,128)S(1)} %get-tuple-element.13), channel_id=1, source_target_pairs={{0,1},{1,0},{2,3},{3,2},{4,5},{5,4},{6,7},{7,6},{8,9},{9,8},{10,11... | collective-permute-start | bytes 122888 | tf_op jit(solution)/shard_map/ppermute | solution.py:329
  3.5 49.3 %all-to-all-start = ((bf16[8,4,80,128]{3,2,1,0:T(8,128)(2,1)}), bf16[8,4,80,128]{3,2,1,0:T(8,128)(2,1)S(1)}, u32[]{:S(2)}, u32[]{:S(2)}) async-start(bf16[8,4,80,128]{3,2,1,0:T(8,128)(2,1)} %bitcast.6), calls=%async_computation | async-start | bytes 1310720 | tf_op jit(solution)/shard_map/all_to_all | solution.py:345
  10.5 17.0 %collective-permute-start.1 = (f32[40,256]{1,0:T(8,128)S(1)}, f32[40,256]{1,0:T(8,128)S(1)}, u32[]{:S(2)}, u32[]{:S(2)}) collective-permute-start(f32[40,256]{1,0:T(8,128)S(1)} %add.27), channel_id=1, source_target_pairs={{0,24},{1,25},{2,26},{3,27},{4,28},{5,29},{6,30},{7,31},{8,16},{9,... | collective-permute-start | bytes 122888 | tf_op jit(solution)/shard_map/ppermute | solution.py:329
  14.3 13.2 %collective-permute-start.2 = (f32[40,256]{1,0:T(8,128)S(1)}, f32[40,256]{1,0:T(8,128)S(1)}, u32[]{:S(2)}, u32[]{:S(2)}) collective-permute-start(f32[40,256]{1,0:T(8,128)S(1)} %add.27), channel_id=1, source_target_pairs={{0,8},{1,9},{2,10},{3,11},{4,12},{5,13},{6,14},{7,15},{8,0},{9,1},... | collective-permute-start | bytes 122888 | tf_op jit(solution)/shard_map/ppermute | solution.py:329
  14.3 17.5 %collective-permute-start.3 = (f32[40,256]{1,0:T(8,128)S(1)}, f32[40,256]{1,0:T(8,128)S(1)}, u32[]{:S(2)}, u32[]{:S(2)}) collective-permute-start(f32[40,256]{1,0:T(8,128)S(1)} %add.27), channel_id=1, source_target_pairs={{0,16},{1,17},{2,18},{3,19},{4,20},{5,21},{6,22},{7,23},{8,24},{9,... | collective-permute-start | bytes 122888 | tf_op jit(solution)/shard_map/ppermute | solution.py:329
  31.9 4.1 %collective-permute-start.4 = (f32[40,256]{1,0:T(8,128)S(1)}, f32[40,256]{1,0:T(8,128)S(1)}, u32[]{:S(2)}, u32[]{:S(2)}) collective-permute-start(f32[40,256]{1,0:T(8,128)S(1)} %add_add_fusion), channel_id=1, source_target_pairs={{0,4},{1,5},{2,6},{3,7},{4,0},{5,1},{6,2},{7,3},{8,12},{9,13},{10,... | collective-permute-start | bytes 122888 | tf_op jit(solution)/shard_map/ppermute | solution.py:329
  35.9 4.0 %collective-permute-start.5 = (f32[40,256]{1,0:T(8,128)S(1)}, f32[40,256]{1,0:T(8,128)S(1)}, u32[]{:S(2)}, u32[]{:S(2)}) collective-permute-start(f32[40,256]{1,0:T(8,128)S(1)} %add.31), channel_id=1, source_target_pairs={{0,2},{1,3},{2,0},{3,1},{4,6},{5,7},{6,4},{7,5},{8,10},{9,11},{10,... | collective-permute-start | bytes 122888 | tf_op jit(solution)/shard_map/ppermute | solution.py:329
  39.9 1.2 %collective-permute-start.6 = (f32[40,256]{1,0:T(8,128)S(1)}, f32[40,256]{1,0:T(8,128)S(1)}, u32[]{:S(2)}, u32[]{:S(2)}) collective-permute-start(f32[40,256]{1,0:T(8,128)S(1)} %add.32.mine_ref), channel_id=1, source_target_pairs={{0,1},{1,0},{2,3},{3,2},{4,5},{5,4},{6,7},{7,6},{8,9},{9,8},{10,11... | collective-permute-start | bytes 122888 | tf_op jit(solution)/shard_map/ppermute | solution.py:329

commit v7 on v5

--- a/solution.py
+++ b/solution.py
@@ -106,7 +106,8 @@
     copies[-1].wait()
     if pixels == LANES and LANES % size == 0 and count % LANES == 0:
         for level in range(levels):
-            grid_ref[level] = state_ref[:, level].astype(f32).reshape(members * regions, pixels)
+            grid = state_ref[:, level].astype(f32).reshape(members * regions, pixels)
+            grid_ref[level, : members * regions] = grid
         together = LANES // size
         tiles = []
         for tile in range(count // LANES):
@@ -302,7 +303,7 @@
                 piece = value[:, pixels * i : pixels * i + pixels]
                 row_ref[s, pl.ds(level, members, stride=levels), :] = piece
         for s in group:
-            piece = row_ref[s].reshape(members, levels, pixels).astype(bf16)
+            piece = row_ref[s, : members * levels].reshape(members, levels, pixels).astype(bf16)
             stage_ref[:, :, pixels * s : pixels * s + pixels] = piece
         span = pl.ds(part * each * pixels, each * pixels)
         copies.append(
@@ -391,7 +392,7 @@
         + [pltpu.VMEM(x.shape, x.dtype) for x in tables]
         + [
             pltpu.SemaphoreType.DMA((11,)),
-            pltpu.VMEM((levels, members * local.shape[2], pixels), f32),
+            pltpu.VMEM((levels, (members + 1) * local.shape[2], pixels), f32),
         ],
         compiler_params=pltpu.CompilerParams(vmem_limit_bytes=24 * 2**20),
     )(
@@ -423,7 +424,7 @@
             in_specs=[vmem] * 3,
             out_specs=pl.BlockSpec(memory_space=pltpu.HBM),
             scratch_shapes=[
-                pltpu.VMEM((region_count, members * levels, pixels), f32),
+                pltpu.VMEM((region_count, (members + 2) * levels, pixels), f32),
                 pltpu.VMEM((members, levels, pixels * region_count), bf16),
                 pltpu.SemaphoreType.DMA((2 if region_count % 2 == 0 else 1,)),
             ],

time: 54.6 us -> 54.6 us (level)
  no operation moved by 1% of the time
where the time goes in v7:
time: 54.6 us; the launch traced here: 54.4 us
  waiting for transfers between devices  23.2 us (42%)
  Pallas kernels  15.1 us (28%)
  starting transfers between devices  14.9 us (27%)
  local copies, waits for them, and re-layouts  1.09 us (2%)
    ppermute x7, waiting for transfers between devices, swap(): return lax.ppermute(x, BOTH, [(i, i ^ k) for i in range(devices)])  23.2 us
    pallas_call x1, Pallas kernels, body(): pl.pallas_call(functools.partial(filter_kernel, members, batches), out_sh...  11.7 us
    ppermute x7, starting transfers between devices, swap(): return lax.ppermute(x, BOTH, [(i, i ^ k) for i in range(devices)])  7.99 us
    all_to_all x1, starting transfers between devices, exchange(): lax.all_to_all(state, 'region', split_axis=0, concat_axis=0, tiled=True)  6.94 us
    pallas_call x1, Pallas kernels, body(): pl.pallas_call(prior_kernel, out_shape=(jax.ShapeDtypeStruct((half, count...  2.04 us
    pallas_call x1, Pallas kernels, body(): pl.pallas_call(apply_kernel, out_shape=jax.ShapeDtypeStruct((members, lev...  1.38 us
    unnamed x3, local copies, waits for them, and re-layouts  1.09 us
  transfers between devices with their start and end apart: 8, of which 5 were waited for; matrix products, arithmetic and copies ran while one was open for 2% of the time, Pallas kernels for 21%

profile of v7, /device:TPU:0, one launch (start us, length us, event | category | flops | bytes accessed | tf_op | source)
XLA Modules:
  0.0 54.4 jit_solution(14689385212003038645)
XLA Ops:
  0.0 0.0 copy-start
  0.0 2.0 %shard_map.100 = (f32[40,256]{1,0:T(8,128)S(1)}, f32[40,256]{1,0:T(8,128)S(1)}, f32[8,256]{1,0:T(8,128)S(1)}) custom-call(s32[1]{0:T(128)} %bitcast.2.first_ref, s32[1]{0:T(128)} %bitcast.1.half_ref, f32[4]{0:T(128)} %refs_0_.1, f32[4]{0:T(128)} %refs_1_.1, s32[4]{0:T(128)} %refs_3_.1, s32[4]{0:T(128)} %refs_3_.1, s32[8]{0:T(128)} %refs_4_.1, ...), custom_call_target="tpu_custom_call" | custom-call | tf_op jit(solution)/shard_map/pallas_call | solution.py:382
  2.1 0.6 %collective-permute-start = (f32[40,256]{1,0:T(8,128)S(1)}, f32[40,256]{1,0:T(8,128)S(1)}, u32[]{:S(2)}, u32[]{:S(2)}) collective-permute-start(f32[40,256]{1,0:T(8,128)S(1)} %get-tuple-element.13), channel_id=1, source_target_pairs={{0,1},{1,0},{2,3},{3,2},{4,5},{5,4},{6,7},{7,6},{8,9},{9,8},{10,11... | collective-permute-start | bytes 122888 | tf_op jit(solution)/shard_map/ppermute | solution.py:321
  2.6 0.0 copy-done
  2.6 1.1 %copy.16 = bf16[80,4,128,8]{2,0,1,3:T(8,128)(2,1)} copy(bf16[80,4,128,8]{2,3,1,0:T(8,128)(2,1)S(1)} %copy-done) | data formatting | bytes 1310720 | tf_op args[0]
  3.7 0.0 collective-permute-done
  3.7 6.9 %all-to-all-start = ((bf16[8,4,80,128]{3,2,1,0:T(8,128)(2,1)}), bf16[8,4,80,128]{3,2,1,0:T(8,128)(2,1)S(1)}, u32[]{:S(2)}, u32[]{:S(2)}) async-start(bf16[8,4,80,128]{3,2,1,0:T(8,128)(2,1)} %bitcast.6), calls=%async_computation | async-start | bytes 1310720 | tf_op jit(solution)/shard_map/all_to_all | solution.py:337
  10.7 3.8 %collective-permute-start.1 = (f32[40,256]{1,0:T(8,128)S(1)}, f32[40,256]{1,0:T(8,128)S(1)}, u32[]{:S(2)}, u32[]{:S(2)}) collective-permute-start(f32[40,256]{1,0:T(8,128)S(1)} %add.27), channel_id=1, source_target_pairs={{0,24},{1,25},{2,26},{3,27},{4,28},{5,29},{6,30},{7,31},{8,16},{9,... | collective-permute-start | bytes 122888 | tf_op jit(solution)/shard_map/ppermute | solution.py:321
  14.5 0.0 collective-permute-start.2
  14.5 0.6 %collective-permute-start.3 = (f32[40,256]{1,0:T(8,128)S(1)}, f32[40,256]{1,0:T(8,128)S(1)}, u32[]{:S(2)}, u32[]{:S(2)}) collective-permute-start(f32[40,256]{1,0:T(8,128)S(1)} %add.27), channel_id=1, source_target_pairs={{0,8},{1,9},{2,10},{3,11},{4,12},{5,13},{6,14},{7,15},{8,0},{9,1},... | collective-permute-start | bytes 122888 | tf_op jit(solution)/shard_map/ppermute | solution.py:321
  15.1 12.6 %collective-permute-done.1 = f32[40,256]{1,0:T(8,128)S(1)} collective-permute-done((f32[40,256]{1,0:T(8,128)S(1)}, f32[40,256]{1,0:T(8,128)S(1)}, u32[]{:S(2)}, u32[]{:S(2)}) %collective-permute-start.1) | collective-permute-done | bytes 40992 | tf_op jit(solution)/shard_map/ppermute | solution.py:321
  27.6 4.4 %collective-permute-done.2 = f32[40,256]{1,0:T(8,128)S(1)} collective-permute-done((f32[40,256]{1,0:T(8,128)S(1)}, f32[40,256]{1,0:T(8,128)S(1)}, u32[]{:S(2)}, u32[]{:S(2)}) %collective-permute-start.2) | collective-permute-done | bytes 40992 | tf_op jit(solution)/shard_map/ppermute | solution.py:321
  32.0 0.0 collective-permute-done.3
  32.0 1.5 %collective-permute-start.4 = (f32[40,256]{1,0:T(8,128)S(1)}, f32[40,256]{1,0:T(8,128)S(1)}, u32[]{:S(2)}, u32[]{:S(2)}) collective-permute-start(f32[40,256]{1,0:T(8,128)S(1)} %add_add_fusion), channel_id=1, source_target_pairs={{0,4},{1,5},{2,6},{3,7},{4,0},{5,1},{6,2},{7,3},{8,12},{9,13},{10,... | collective-permute-start | bytes 122888 | tf_op jit(solution)/shard_map/ppermute | solution.py:321
  33.6 2.5 %collective-permute-done.4 = f32[40,256]{1,0:T(8,128)S(1)} collective-permute-done((f32[40,256]{1,0:T(8,128)S(1)}, f32[40,256]{1,0:T(8,128)S(1)}, u32[]{:S(2)}, u32[]{:S(2)}) %collective-permute-start.4) | collective-permute-done | bytes 40992 | tf_op jit(solution)/shard_map/ppermute | solution.py:321
  36.1 1.5 %collective-permute-start.5 = (f32[40,256]{1,0:T(8,128)S(1)}, f32[40,256]{1,0:T(8,128)S(1)}, u32[]{:S(2)}, u32[]{:S(2)}) collective-permute-start(f32[40,256]{1,0:T(8,128)S(1)} %add.31), channel_id=1, source_target_pairs={{0,2},{1,3},{2,0},{3,1},{4,6},{5,7},{6,4},{7,5},{8,10},{9,11},{10,... | collective-permute-start | bytes 122888 | tf_op jit(solution)/shard_map/ppermute | solution.py:321
  37.6 2.5 %collective-permute-done.5 = f32[40,256]{1,0:T(8,128)S(1)} collective-permute-done((f32[40,256]{1,0:T(8,128)S(1)}, f32[40,256]{1,0:T(8,128)S(1)}, u32[]{:S(2)}, u32[]{:S(2)}) %collective-permute-start.5) | collective-permute-done | bytes 40992 | tf_op jit(solution)/shard_map/ppermute | solution.py:321
  40.1 0.0 collective-permute-start.6
  40.1 1.2 %collective-permute-done.6.other_ref = f32[40,256]{1,0:T(8,128)S(1)} collective-permute-done((f32[40,256]{1,0:T(8,128)S(1)}, f32[40,256]{1,0:T(8,128)S(1)}, u32[]{:S(2)}, u32[]{:S(2)}) %collective-permute-start.6) | collective-permute-done | bytes 40992 | tf_op jit(solution)/shard_map/ppermute | solution.py:321
  41.4 11.7 %shard_map.101 = (bf16[80,128]{1,0:T(8,128)(2,1)S(1)}, bf16[80,128]{1,0:T(8,128)(2,1)S(1)}) custom-call(s32[1]{0:T(128)} %bitcast.own_ref, s32[1]{0:T(128)} %bitcast.1.half_ref, f32[40,256]{1,0:T(8,128)S(1)} %add.32.mine_ref, f32[40,256]{1,0:T(8,128)S(1)} %collective-permute-done.6.other_ref, f32[8,256]{1,0:T(8,128)S(1)} %get-tuple-element.15.aux_ref), custom_call_target="tpu_custom_call" | custom-call | flops 1000000000 | bytes 1000000 | tf_op jit(solution)/shard_map/pallas_call | solution.py:404
  53.1 0.0 all-to-all-done.whole_ref
  53.1 1.4 %shard_map.102 = bf16[80,4,1024]{2,1,0:T(4,128)(2,1)} custom-call(bf16[80,128]{1,0:T(8,128)(2,1)S(1)} %get-tuple-element.16.high_ref, bf16[80,128]{1,0:T(8,128)(2,1)S(1)} %get-tuple-element.17.low_ref, bf16[8,4,80,128]{3,2,1,0:T(8,128)(2,1)S(1)} %all-to-all-done.whole_ref), custom_call_target="tpu_custom_call" | custom-call | tf_op jit(solution)/shard_map/pallas_call | solution.py:421
  (4 shorter events, 0.0 us)
Async XLA Ops:
  0.0 2.6 %copy-start = (bf16[80,4,128,8]{2,3,1,0:T(8,128)(2,1)S(1)}, bf16[80,4,128,8]{2,3,1,0:T(8,128)(2,1)}, u32[]{:S(2)}) copy-start(bf16[80,4,128,8]{2,3,1,0:T(8,128)(2,1)} %param.10) | copy-start | bytes 1966084
  2.1 1.7 %collective-permute-start = (f32[40,256]{1,0:T(8,128)S(1)}, f32[40,256]{1,0:T(8,128)S(1)}, u32[]{:S(2)}, u32[]{:S(2)}) collective-permute-start(f32[40,256]{1,0:T(8,128)S(1)} %get-tuple-element.13), channel_id=1, source_target_pairs={{0,1},{1,0},{2,3},{3,2},{4,5},{5,4},{6,7},{7,6},{8,9},{9,8},{10,11... | collective-permute-start | bytes 122888 | tf_op jit(solution)/shard_map/ppermute | solution.py:321
  3.7 49.3 %all-to-all-start = ((bf16[8,4,80,128]{3,2,1,0:T(8,128)(2,1)}), bf16[8,4,80,128]{3,2,1,0:T(8,128)(2,1)S(1)}, u32[]{:S(2)}, u32[]{:S(2)}) async-start(bf16[8,4,80,128]{3,2,1,0:T(8,128)(2,1)} %bitcast.6), calls=%async_computation | async-start | bytes 1310720 | tf_op jit(solution)/shard_map/all_to_all | solution.py:337
  10.7 17.0 %collective-permute-start.1 = (f32[40,256]{1,0:T(8,128)S(1)}, f32[40,256]{1,0:T(8,128)S(1)}, u32[]{:S(2)}, u32[]{:S(2)}) collective-permute-start(f32[40,256]{1,0:T(8,128)S(1)} %add.27), channel_id=1, source_target_pairs={{0,24},{1,25},{2,26},{3,27},{4,28},{5,29},{6,30},{7,31},{8,16},{9,... | collective-permute-start | bytes 122888 | tf_op jit(solution)/shard_map/ppermute | solution.py:321
  14.5 17.6 %collective-permute-start.2 = (f32[40,256]{1,0:T(8,128)S(1)}, f32[40,256]{1,0:T(8,128)S(1)}, u32[]{:S(2)}, u32[]{:S(2)}) collective-permute-start(f32[40,256]{1,0:T(8,128)S(1)} %add.27), channel_id=1, source_target_pairs={{0,16},{1,17},{2,18},{3,19},{4,20},{5,21},{6,22},{7,23},{8,24},{9,... | collective-permute-start | bytes 122888 | tf_op jit(solution)/shard_map/ppermute | solution.py:321
  14.5 17.6 %collective-permute-start.3 = (f32[40,256]{1,0:T(8,128)S(1)}, f32[40,256]{1,0:T(8,128)S(1)}, u32[]{:S(2)}, u32[]{:S(2)}) collective-permute-start(f32[40,256]{1,0:T(8,128)S(1)} %add.27), channel_id=1, source_target_pairs={{0,8},{1,9},{2,10},{3,11},{4,12},{5,13},{6,14},{7,15},{8,0},{9,1},... | collective-permute-start | bytes 122888 | tf_op jit(solution)/shard_map/ppermute | solution.py:321
  32.0 4.1 %collective-permute-start.4 = (f32[40,256]{1,0:T(8,128)S(1)}, f32[40,256]{1,0:T(8,128)S(1)}, u32[]{:S(2)}, u32[]{:S(2)}) collective-permute-start(f32[40,256]{1,0:T(8,128)S(1)} %add_add_fusion), channel_id=1, source_target_pairs={{0,4},{1,5},{2,6},{3,7},{4,0},{5,1},{6,2},{7,3},{8,12},{9,13},{10,... | collective-permute-start | bytes 122888 | tf_op jit(solution)/shard_map/ppermute | solution.py:321
  36.1 4.0 %collective-permute-start.5 = (f32[40,256]{1,0:T(8,128)S(1)}, f32[40,256]{1,0:T(8,128)S(1)}, u32[]{:S(2)}, u32[]{:S(2)}) collective-permute-start(f32[40,256]{1,0:T(8,128)S(1)} %add.31), channel_id=1, source_target_pairs={{0,2},{1,3},{2,0},{3,1},{4,6},{5,7},{6,4},{7,5},{8,10},{9,11},{10,... | collective-permute-start | bytes 122888 | tf_op jit(solution)/shard_map/ppermute | solution.py:321
  40.1 1.2 %collective-permute-start.6 = (f32[40,256]{1,0:T(8,128)S(1)}, f32[40,256]{1,0:T(8,128)S(1)}, u32[]{:S(2)}, u32[]{:S(2)}) collective-permute-start(f32[40,256]{1,0:T(8,128)S(1)} %add.32.mine_ref), channel_id=1, source_target_pairs={{0,1},{1,0},{2,3},{3,2},{4,5},{5,4},{6,7},{7,6},{8,9},{9,8},{10,11... | collective-permute-start | bytes 122888 | tf_op jit(solution)/shard_map/ppermute | solution.py:321
